TPU v7x, 32 devices: a whole 2x2x4 slice. The times are simulated.
32 devices in a mesh: series: 16 (over z, y, core), mp: 2 (over x).
Axes of the slice: x: 2, y: 2, z: 4, core: 2. Of those that a mesh axis runs over, the one named last changes fastest.
Arguments:
- series_in: bfloat16 [256, 256, 768], P('series'), may hold values from -6 to 6
- norm_gain: float32 [768], replicated, may hold values from 0.5 to 1.5
- w_time: bfloat16 [768, 12, 192], P(None, 'mp'), may hold values from -0.375 to 0.375
- w_group: bfloat16 [768, 12, 192], P(None, 'mp'), may hold values from -0.375 to 0.375
- w_gate: bfloat16 [768, 768], P(None, 'mp'), may hold values from -0.4375 to 0.4375
- w_out: bfloat16 [768, 768], P('mp'), may hold values from -0.4375 to 0.4375
- group_of: int32 [256], replicated, may hold values from 0 to 7, as said below
Outputs:
- block_out: bfloat16 [256, 256, 768], P('series', None, 'mp')
Inputs may be any that keep to these rules, and one draw needn't show every extreme that they name: `group_of`: groups are numbered from 0 without gaps; each holds 8 to 64 series, one group exactly 8 and one exactly 64; members are spread over the series at random.
All inputs are finite; a program needn't handle non-finite values.
Results may differ from a plain program's by a relative error of at most 0.015.
Values may be sent and summed in bfloat16 or wider, within the bound.
A program may use at most 128 MiB of HBM per device.

v0:
```python
from functools import partial

import jax
import jax.numpy as jnp
from jax import lax
from jax.sharding import PartitionSpec as P


def rms_norm(series_in, norm_gain):
    values_f = series_in.astype(jnp.float32)
    mean_sq = jnp.mean(values_f * values_f, axis=-1, keepdims=True)
    return (values_f * lax.rsqrt(mean_sq + 1e-06) * norm_gain).astype(jnp.bfloat16)


def time_attend(time_qkv):
    head_size = time_qkv.shape[-1]
    queries = time_qkv[:, :, :, 0]
    keys_in = time_qkv[:, :, :, 1]
    values_in = time_qkv[:, :, :, 2]
    scores = jnp.einsum(
        "bphd,bqhd->bhpq", queries, keys_in, preferred_element_type=jnp.float32
    ) * head_size ** (-0.5)
    weights = jax.nn.softmax(scores, axis=-1).astype(jnp.bfloat16)
    return jnp.einsum(
        "bhpq,bqhd->bphd", weights, values_in, preferred_element_type=jnp.float32
    ).astype(jnp.bfloat16)


def group_patch(patch_qkv, same_group):
    head_size = patch_qkv.shape[-1]
    queries = patch_qkv[:, :, 0]
    keys_in = patch_qkv[:, :, 1]
    values_in = patch_qkv[:, :, 2]
    scores = jnp.einsum(
        "ihd,jhd->hij", queries, keys_in, preferred_element_type=jnp.float32
    ) * head_size ** (-0.5)
    scores = jnp.where(same_group[None], scores, -1e30)
    weights = jax.nn.softmax(scores, axis=-1).astype(jnp.bfloat16)
    return jnp.einsum(
        "hij,jhd->ihd", weights, values_in, preferred_element_type=jnp.float32
    ).astype(jnp.bfloat16)


def per_device(series_in, norm_gain, w_time, w_group, w_gate, w_out, group_of):
    ser_local, patches, width = series_in.shape
    heads_local = w_time.shape[1]
    head_size = w_time.shape[2] // 3
    normed = rms_norm(series_in, norm_gain)
    flat_rows = normed.reshape(ser_local * patches, width)
    time_qkv = jnp.dot(
        flat_rows, w_time.reshape(width, -1), preferred_element_type=jnp.float32
    ).astype(jnp.bfloat16)
    time_qkv = time_qkv.reshape(ser_local, patches, heads_local, 3, head_size)
    time_out = time_attend(time_qkv).reshape(ser_local * patches, heads_local * head_size)
    quarter = width // lax.axis_size("mp")
    own_columns = lax.dynamic_slice_in_dim(normed, lax.axis_index("mp") * quarter, quarter, 2)
    moved = lax.all_to_all(own_columns, "series", split_axis=1, concat_axis=0, tiled=True)
    full_rows = lax.all_gather(moved, "mp", axis=2, tiled=True)
    owned = jnp.dot(
        full_rows.reshape(-1, width), w_group.reshape(width, -1), preferred_element_type=jnp.float32
    ).astype(jnp.bfloat16)
    owned = owned.reshape(full_rows.shape[0], full_rows.shape[1], -1)
    all_series, patch_local = (owned.shape[0], owned.shape[1])
    owned = owned.reshape(all_series, patch_local, heads_local, 3, head_size)
    same_group = group_of[:, None] == group_of[None, :]
    group_out = lax.map(partial(group_patch, same_group=same_group), jnp.moveaxis(owned, 1, 0))
    group_out = jnp.moveaxis(group_out, 0, 1).reshape(
        all_series, patch_local, heads_local * head_size
    )
    returned = lax.all_to_all(group_out, "series", split_axis=0, concat_axis=1, tiled=True)
    returned = returned.reshape(ser_local * patches, heads_local * head_size)
    gate_value = jax.nn.sigmoid(jnp.dot(flat_rows, w_gate, preferred_element_type=jnp.float32))
    merged = (time_out.astype(jnp.float32) + gate_value * returned.astype(jnp.float32)).astype(
        jnp.bfloat16
    )
    head_term = jnp.dot(merged, w_out, preferred_element_type=jnp.float32).reshape(
        ser_local, patches, width
    )
    return lax.psum_scatter(head_term.astype(jnp.bfloat16), "mp", scatter_dimension=2, tiled=True)


def solution(mesh):
    placed = (
        P("series", None, None),
        P(),
        P(None, "mp", None),
        P(None, "mp", None),
        P(None, "mp"),
        P("mp", None),
        P(),
    )
    return jax.shard_map(
        per_device, mesh=mesh, in_specs=placed, out_specs=P("series", None, "mp"), check_vma=False
    )
```

profile of v0, /device:TPU:0, one launch (start us, length us, event | category | flops | bytes accessed | tf_op | source)
XLA Modules:
  0.0 555.5 jit_solution(7793506105752205166)
XLA Ops:
  10.8 6.9 %fusion.21 = bf16[16,256,768]{2,1,0:T(8,128)(2,1)} fusion(bf16[16,256,768]{2,1,0:T(8,128)(2,1)} %param.9, f32[768]{0:T(1024)S(1)} %copy-done.3, f32[16,256]{1,0:T(8,128)S(1)} %add_rsqrt_fusion), kind=kLoop, calls=%fused_computation.31 | loop fusion | flops 12582912 | bytes 12602368 | tf_op jit(solution)/shard_map/convert_element_type | solution.py:12
  21.8 77.4 %all_to_all.27 = bf16[16,256,384]{2,0,1:T(8,128)(2,1)S(1)} all-to-all(bf16[16,256,384]{2,0,1:T(8,128)(2,1)S(1)} %copy.58), channel_id=1, replica_groups=mesh['series'=16,'mp'=2] {'series'}, dimensions={1} | all-to-all | bytes 6291456 | tf_op jit(solution)/shard_map/all_to_all | solution.py:57
  101.8 14.9 %convolution_convert_fusion.2 = bf16[4096,1152]{1,0:T(8,128)(2,1)} fusion(bf16[4096,768]{1,0:T(8,128)(2,1)} %bitcast.120, bf16[768,1152]{0,1:T(8,128)(2,1)S(1)} %bitcast.112), kind=kOutput, calls=%fused_computation.28 | convolution fusion | flops 7252475904 | bytes 17498112 | tf_op jit(solution)/shard_map/dot_general | solution.py:50
  116.7 12.8 %copy.52 = bf16[4096,1152]{0,1:T(8,128)(2,1)} copy(bf16[4096,1152]{1,0:T(8,128)(2,1)} %convolution_convert_fusion.2) | data formatting | bytes 18874368 | tf_op jit(solution)/shard_map/convert_element_type | solution.py:52
  129.5 11.4 %copy.73 = bf16[144,8,16,256]{3,2,1,0:T(8,128)(2,1)} copy(bf16[144,8,16,256]{3,1,2,0:T(8,128)(2,1)} %bitcast.115) | data formatting | bytes 18874368
  140.9 6.8 %fusion.29 = (bf16[16,256,6,1,64]{1,0,4,3,2:T(8,128)(2,1)}, bf16[16,256,6,1,64]{1,0,4,3,2:T(8,128)(2,1)}, bf16[16,256,6,1,64]{1,0,4,3,2:T(8,128)(2,1)}) fusion(bf16[16,256,6,3,64]{1,0,4,3,2:T(8,128)(2,1)} %bitcast.114), kind=kLoop, calls=%fused_computation.48 | loop fusion | bytes 18874368 | tf_op jit(solution)/shard_map/slice | solution.py:19
  147.7 35.1 %all-gather.2.cloned.1.call-done = bf16[256,16,768]{2,1,0:T(8,128)(2,1)} async-done(((bf16[256,16,384]{2,1,0:T(8,128)(2,1)}), bf16[256,16,768]{2,1,0:T(8,128)(2,1)}) %all-gather.2.cloned.1.call-update) | async-done | bytes 6291472 | tf_op jit(solution)/shard_map/all_gather | solution.py:58
  182.8 15.1 %convolution_convert_fusion.1 = bf16[4096,1152]{1,0:T(8,128)(2,1)} fusion(bf16[4096,768]{1,0:T(8,128)(2,1)} %bitcast.132, bf16[768,1152]{0,1:T(8,128)(2,1)S(1)} %bitcast.133), kind=kOutput, calls=%fused_computation.27 | convolution fusion | flops 7252475904 | bytes 17498112 | tf_op jit(solution)/shard_map/dot_general | solution.py:59
  197.9 45.5 %reshape_reshape.3 = bf16[256,16,6,3,64]{4,3,2,1,0:T(4,128)(2,1)} reshape(bf16[4096,1152]{1,0:T(8,128)(2,1)} %convolution_convert_fusion.1) | data formatting | bytes 18874368 | tf_op jit(solution)/shard_map/reshape;reshape | solution.py:64
  243.4 35.7 %copy.61 = bf16[16,256,6,3,64]{1,4,2,3,0:T(8,128)(2,1)} copy(bf16[16,256,6,3,64]{4,3,2,0,1:T(4,128)(2,1)} %bitcast.113) | data formatting | bytes 18874368
  279.1 56.3 %while.11 = (s32[]{:T(128)}, bf16[16,256,6,64]{1,3,2,0:T(8,128)(2,1)}, bf16[16,256,6,3,64]{1,4,2,3,0:T(8,128)(2,1)}, s32[256]{0:T(256)S(1)}, s32[]{:T(128)}) while((s32[]{:T(128)}, bf16[16,256,6,64]{1,3,2,0:T(8,128)(2,1)}, bf16[16,256,6,3,64]{1,4,2,3,0:T(8,128)(2,1)}, s32[256]{0:T(256)S(1)}, s32[]{:T(128)}) %tuple.35), condition=%wide.region_6.7_spmd.clone, body=%wide.region_3.6_spmd.clone.sunk | while | flops 154699776 | bytes 2569793 | solution.py:66
  335.4 5.1 copy.62
  340.4 5.6 %all-to-all-start.1 = ((bf16[256,16,384]{2,1,0:T(8,128)(2,1)}), bf16[256,16,384]{2,1,0:T(8,128)(2,1)}, u32[]{:S(2)}, u32[]{:S(2)}) async-start(bf16[256,16,384]{2,1,0:T(8,128)(2,1)} %copy.62), calls=%async_computation.1 | async-start | bytes 6291456 | tf_op jit(solution)/shard_map/all_to_all | solution.py:70
  346.1 16.3 %fusion.26 = f32[16,6,256,256]{2,3,1,0:T(8,128)} fusion(bf16[16,256,6,1,64]{1,0,4,3,2:T(8,128)(2,1)} %get-tuple-element.65, bf16[16,256,6,1,64]{1,0,4,3,2:T(8,128)(2,1)} %get-tuple-element.64), kind=kOutput, calls=%fused_computation.41 | convolution fusion | flops 805306368 | bytes 31457280 | tf_op jit(solution)/shard_map/bphd,bqhd->bhpq/dot_general | solution.py:20
  362.4 27.1 %fusion.30 = (f32[16,6,256]{2,1,0:T(8,128)S(1)}, f32[16,6,256,256]{2,3,1,0:T(8,128)}) fusion(f32[16,6,256,256]{2,3,1,0:T(8,128)} %fusion.26), kind=kOutput, calls=%fused_computation.49 | output fusion | flops 25166080 | bytes 50429952 | tf_op jit(solution)/shard_map/sub | solution.py:23
  389.5 14.9 %convert_bitcast_fusion.1 = f32[16,256,6,64]{1,3,2,0:T(8,128)} fusion(f32[16,6,256,256]{2,3,1,0:T(8,128)} %get-tuple-element.67, f32[16,6,256]{2,1,0:T(8,128)S(1)} %get-tuple-element.66, bf16[16,256,6,1,64]{1,0,4,3,2:T(8,128)(2,1)} %get-tuple-element.63), kind=kOutput, calls=%fused_computation.39 | convolution fusion | flops 821035008 | bytes 34701312 | tf_op jit(solution)/shard_map/bhpq,bqhd->bphd/dot_general | solution.py:24
  404.4 6.4 %copy.57 = f32[16,256,6,64]{1,0,3,2:T(8,128)S(1)} copy(f32[16,256,6,64]{1,3,2,0:T(8,128)} %convert_bitcast_fusion.1) | data formatting | bytes 12582912 | tf_op jit(solution)/shard_map/convert_element_type | solution.py:73
  410.8 9.0 %copy.74 = f32[48,8,16,256]{3,1,2,0:T(8,128)} copy(f32[48,8,16,256]{3,2,1,0:T(8,128)S(1)} %bitcast.117) | data formatting | bytes 12582912
  419.8 6.6 %copy.64 = f32[4096,384]{1,0:T(8,128)} copy(f32[4096,384]{0,1:T(8,128)} %bitcast.118) | data formatting | bytes 12582912 | tf_op jit(solution)/shard_map/convert_element_type | solution.py:73
  437.0 5.2 convolution_convert_fusion.3
  442.2 9.3 %copy.68 = bf16[16,256,768]{1,0,2:T(8,128)(2,1)} copy(bf16[16,256,768]{2,1,0:T(8,128)(2,1)} %bitcast.129) | data formatting | bytes 12582912
  451.5 9.6 %copy.75 = bf16[96,8,16,256]{3,1,2,0:T(8,128)(2,1)} copy(bf16[96,8,16,256]{3,2,1,0:T(8,128)(2,1)} %bitcast.119) | data formatting | bytes 12582912
  461.2 77.6 %reduce-scatter.4.cloned.1.call-done = bf16[384,4096]{1,0:T(8,128)(2,1)} async-done(((bf16[768,4096]{1,0:T(8,128)(2,1)}), bf16[384,4096]{1,0:T(8,128)(2,1)}) %reduce-scatter.4.cloned.1.call-update) | async-done | bytes 3145744
  543.5 4.9 copy.69
  (103 shorter events, 82.3 us)
Async XLA Ops:
  6.5 95.2 %copy-start = (bf16[768,6,192]{0,2,1:T(8,128)(2,1)S(1)}, bf16[768,6,192]{0,2,1:T(8,128)(2,1)}, u32[]{:S(2)}) copy-start(bf16[768,6,192]{0,2,1:T(8,128)(2,1)} %param.11) | copy-start | bytes 5308420
  6.5 4.3 copy-start.3
  6.5 176.3 %all-gather.2.cloned.1.call-start = ((), (), s32[]{:S(2)}) async-start(), calls=%async_computation.3 | async-start | bytes 9437184 | tf_op jit(solution)/shard_map/all_gather | solution.py:58
  140.9 41.9 %copy-start.4 = (bf16[768,6,192]{0,2,1:T(8,128)(2,1)S(1)}, bf16[768,6,192]{0,2,1:T(8,128)(2,1)}, u32[]{:S(2)}) copy-start(bf16[768,6,192]{0,2,1:T(8,128)(2,1)} %param.12) | copy-start | bytes 5308420
  243.4 35.7 %copy-start.2 = (s32[256]{0:T(256)S(1)}, s32[256]{0:T(256)}, u32[]{:S(2)}) copy-start(s32[256]{0:T(256)} %param.15) | copy-start | bytes 3076
  340.4 85.9 %all-to-all-start.1 = ((bf16[256,16,384]{2,1,0:T(8,128)(2,1)}), bf16[256,16,384]{2,1,0:T(8,128)(2,1)}, u32[]{:S(2)}, u32[]{:S(2)}) async-start(bf16[256,16,384]{2,1,0:T(8,128)(2,1)} %copy.62), calls=%async_computation.1 | async-start | bytes 6291456 | tf_op jit(solution)/shard_map/all_to_all | solution.py:70
  346.1 192.7 %reduce-scatter.4.cloned.1.call-start = ((), (), s32[]{:S(2)}) async-start(), calls=%async_computation.4 | async-start | bytes 9437184
  426.4 3.5 slice-start
  426.4 4.4 slice-start.2
  429.1 2.5 slice-start.1
  429.1 3.1 slice-start.3
  429.1 3.1 copy-start.5
  432.2 4.8 copy-start.6
  538.8 9.7 %copy-start.1 = (bf16[768,6,192]{0,2,1:T(8,128)(2,1)S(1)}, bf16[768,6,192]{0,2,1:T(8,128)(2,1)}, u32[]{:S(2)}) copy-start(bf16[768,6,192]{0,2,1:T(8,128)(2,1)} %param.11) | copy-start | bytes 5308420
Sparse Core Ops, SparseCore 0:
  101.9 80.8 all-gather.1
  461.3 77.4 reduce-scatter.3
where the time goes:
time: 564 us; the launch traced here: 556 us
  local copies, waits for them, and re-layouts  195 us (35%)
  waiting for transfers between devices  113 us (20%)
  matrix products  108 us (19%)
  blocking collectives  77.4 us (14%)
  other arithmetic  42.5 us (8%)
  between operations  13.8 us (2%)
  starting transfers between devices  5.69 us (1%)
    unnamed x29, local copies, waits for them, and re-layouts  87.1 us
    unnamed x3, waiting for transfers between devices  77.7 us
    all_to_all x1, blocking collectives, per_device(): lax.all_to_all(own_columns, 'series', split_axis=1, concat_axis=0, tiled=...  77.4 us
    another operation x1, local copies, waits for them, and re-layouts, per_device(): owned = owned.reshape(all_series, patch_local, heads_local, 3, head_size)  45.5 us
    all_gather x1, waiting for transfers between devices, per_device(): full_rows = lax.all_gather(moved, 'mp', axis=2, tiled=True)  35.1 us
    sub x1, other arithmetic, time_attend(): weights = jax.nn.softmax(scores, axis=-1).astype(jnp.bfloat16)  27.1 us
    dot_general x16, matrix products, group_patch(): jnp.einsum('hij,jhd->ihd', weights, values_in, preferred_element_type=jnp...  25.6 us
    squeeze x16, local copies, waits for them, and re-layouts, per_device(): lax.map(partial(group_patch, same_group=same_group), jnp.moveaxis(owned,...  17.7 us
  transfers between devices with their start and end apart: 3, of which 2 were waited for; matrix products, arithmetic and copies ran while one was open for 23% of the time, Pallas kernels for 0%

commit v1 on v0

--- a/solution.py
+++ b/solution.py
@@ -3,13 +3,203 @@
 import jax
 import jax.numpy as jnp
 from jax import lax
+from jax.experimental import pallas as pl
+from jax.experimental.pallas import tpu as pltpu
 from jax.sharding import PartitionSpec as P
+
+CHUNKS = 1
+VMEM_BYTES = 60 * 1024 * 1024
 
 
 def rms_norm(series_in, norm_gain):
     values_f = series_in.astype(jnp.float32)
     mean_sq = jnp.mean(values_f * values_f, axis=-1, keepdims=True)
     return (values_f * lax.rsqrt(mean_sq + 1e-06) * norm_gain).astype(jnp.bfloat16)
+
+
+def attend_pair(queries, keys_in, values_in, bias, head_size):
+    rows = queries.shape[0]
+    lane = lax.broadcasted_iota(jnp.int32, queries.shape, 1)
+    first = lane < head_size
+    zero = jnp.zeros_like(queries)
+    ones = jnp.ones_like(values_in)
+    extended = jnp.concatenate([values_in, ones], axis=1)
+    outs = []
+    for own in (jnp.where(first, queries, zero), jnp.where(first, zero, queries)):
+        scores = lax.dot_general(
+            own, keys_in, (((1,), (1,)), ((), ())), preferred_element_type=jnp.float32
+        )
+        if bias is not None:
+            scores = scores + bias
+        top = jnp.max(scores, axis=1, keepdims=True)
+        weights = jnp.exp(scores - top).astype(jnp.bfloat16)
+        outs.append(jnp.dot(weights, extended, preferred_element_type=jnp.float32))
+    pair = values_in.shape[1]
+    sums = jnp.where(first, outs[0][:, pair:], outs[1][:, pair:])
+    tops = jnp.where(first, outs[0][:, :pair], outs[1][:, :pair])
+    return tops / sums
+
+
+def time_kernel(x_ref, gain_ref, w_ref, out_ref, *, head_size):
+    normed = rms_norm(x_ref[0], gain_ref[...])
+    width = out_ref.shape[-1]
+    pair = 2 * head_size
+    scale = head_size ** (-0.5)
+    qkv = jnp.dot(normed, w_ref[...], preferred_element_type=jnp.float32)
+    queries = (qkv[:, :width].astype(jnp.bfloat16) * scale).astype(jnp.bfloat16)
+    keys_in = qkv[:, width : 2 * width].astype(jnp.bfloat16)
+    values_in = qkv[:, 2 * width :].astype(jnp.bfloat16)
+    for at in range(0, width, pair):
+        cut = slice(at, at + pair)
+        out_ref[0, :, cut] = attend_pair(
+            queries[:, cut], keys_in[:, cut], values_in[:, cut], None, head_size
+        ).astype(jnp.bfloat16)
+
+
+def group_kernel(x_ref, w_ref, row_ref, col_ref, out_ref, *, head_size):
+    sources, _, ser_local, depth = x_ref.shape
+    members = w_ref.shape[0]
+    width = w_ref.shape[2] // 4
+    pair = 2 * head_size
+    scale = head_size ** (-0.5)
+    rows = x_ref[...].reshape(sources * ser_local, depth)
+    bias = jnp.where(row_ref[...] == col_ref[...], 0.0, -1e30).astype(jnp.float32)
+    for member in range(members):
+        made = jnp.dot(rows, w_ref[member], preferred_element_type=jnp.float32)
+        queries = (made[:, :width].astype(jnp.bfloat16) * scale).astype(jnp.bfloat16)
+        keys_in = made[:, width : 2 * width].astype(jnp.bfloat16)
+        values_in = made[:, 2 * width : 3 * width].astype(jnp.bfloat16)
+        gate = jax.nn.sigmoid(made[:, 3 * width :])
+        for at in range(0, width, pair):
+            cut = slice(at, at + pair)
+            got = attend_pair(queries[:, cut], keys_in[:, cut], values_in[:, cut], bias, head_size)
+            got = (gate[:, cut] * got).astype(jnp.bfloat16)
+            to = member * width + at
+            out_ref[:, 0, :, to : to + pair] = got.reshape(sources, ser_local, pair)
+
+
+def join_kernel(group_ref, own_ref, other_ref, w_ref, keep_ref, send_ref):
+    me = lax.axis_index("mp")
+    block, ser_local, width = group_ref.shape
+    half = width // 2
+    group = jnp.swapaxes(group_ref[...].astype(jnp.float32), 0, 1).reshape(ser_local * block, width)
+    own = own_ref[...].reshape(ser_local * block, half).astype(jnp.float32)
+    other = other_ref[...].reshape(ser_local * block, half).astype(jnp.float32)
+    is_low = me == 0
+    low = jnp.where(is_low, own, other)
+    high = jnp.where(is_low, other, own)
+    merged = (jnp.concatenate([low, high], axis=1) + group).astype(jnp.bfloat16)
+    result = jnp.dot(merged, w_ref[...], preferred_element_type=jnp.float32).astype(jnp.bfloat16)
+    result = result.reshape(ser_local, block, width)
+    low, high = result[:, :, :half], result[:, :, half:]
+    keep_ref[...] = jnp.where(is_low, low, high)
+    send_ref[...] = jnp.where(is_low, high, low)
+
+
+def join_heads(weight):
+    depth, heads, triple = weight.shape
+    split = weight.reshape(depth, heads, 3, triple // 3)
+    return jnp.swapaxes(split, 1, 2).reshape(depth, heads * triple)
+
+
+def split_patches(series_in, norm_gain, w_time, w_group, w_gate, w_out, group_of):
+    ser_local, patches, depth = series_in.shape
+    heads_local = w_time.shape[1]
+    head_size = w_time.shape[2] // 3
+    width = heads_local * head_size
+    total = heads_local * head_size * 2
+    ns, nm = lax.axis_size("series"), lax.axis_size("mp")
+    me = lax.axis_index("mp")
+    half = patches // nm
+    each = half // ns
+    n_series = group_of.shape[0]
+    params = lambda: pltpu.CompilerParams(vmem_limit_bytes=VMEM_BYTES)
+
+    own_half = lax.dynamic_slice_in_dim(series_in, me * half, half, 1)
+    send = rms_norm(own_half, norm_gain)
+    send = jnp.transpose(send.reshape(ser_local, ns, each, depth), (1, 2, 0, 3))
+
+    w_mix = jnp.concatenate([join_heads(w_group), w_gate], axis=1)
+    w_mix = lax.all_gather(w_mix, "mp", axis=0)
+    w_full = lax.all_gather(w_out, "mp", axis=0, tiled=True)
+
+    step = each // CHUNKS
+    received = []
+    for c in range(CHUNKS):
+        piece = send[:, c * step : (c + 1) * step]
+        received.append(lax.all_to_all(piece, "series", split_axis=0, concat_axis=0, tiled=True))
+
+    time_out = pl.pallas_call(
+        partial(time_kernel, head_size=head_size),
+        grid=(ser_local,),
+        in_specs=[
+            pl.BlockSpec((1, patches, depth), lambda i: (i, 0, 0)),
+            pl.BlockSpec((1, depth), lambda i: (0, 0)),
+            pl.BlockSpec((depth, 3 * width), lambda i: (0, 0)),
+        ],
+        out_specs=pl.BlockSpec((1, patches, width), lambda i: (i, 0, 0)),
+        out_shape=jax.ShapeDtypeStruct((ser_local, patches, width), jnp.bfloat16),
+        compiler_params=params(),
+        name="time_path",
+        cost_estimate=pl.CostEstimate(
+            flops=2 * ser_local * patches * (depth * 3 * width + 4 * patches * width),
+            bytes_accessed=ser_local * patches * (depth + width) * 2,
+            transcendentals=ser_local * heads_local * patches * patches,
+        ),
+    )(series_in, norm_gain.reshape(1, depth), join_heads(w_time))
+
+    swap = [(i, nm - 1 - i) for i in range(nm)]
+    time_send = lax.dynamic_slice_in_dim(time_out, (nm - 1 - me) * half, half, 1)
+    time_other = lax.ppermute(time_send, "mp", swap)
+    time_own = lax.dynamic_slice_in_dim(time_out, me * half, half, 1)
+
+    returned = []
+    for c in range(CHUNKS):
+        group_out = pl.pallas_call(
+            partial(group_kernel, head_size=head_size),
+            grid=(step,),
+            in_specs=[
+                pl.BlockSpec((ns, 1, ser_local, depth), lambda i: (0, i, 0, 0)),
+                pl.BlockSpec((nm, depth, 4 * width), lambda i: (0, 0, 0)),
+                pl.BlockSpec((n_series, 1), lambda i: (0, 0)),
+                pl.BlockSpec((1, n_series), lambda i: (0, 0)),
+            ],
+            out_specs=pl.BlockSpec((ns, 1, ser_local, total), lambda i: (0, i, 0, 0)),
+            out_shape=jax.ShapeDtypeStruct((ns, step, ser_local, total), jnp.bfloat16),
+            compiler_params=params(),
+            name="group_path",
+            cost_estimate=pl.CostEstimate(
+                flops=2 * step * n_series * (depth * 4 * total + 4 * n_series * total),
+                bytes_accessed=step * n_series * (depth + total) * 2,
+                transcendentals=step * nm * heads_local * n_series * n_series,
+            ),
+        )(received[c], w_mix, group_of.reshape(n_series, 1), group_of.reshape(1, n_series))
+        returned.append(
+            lax.all_to_all(group_out, "series", split_axis=0, concat_axis=0, tiled=True)
+        )
+
+    back = jnp.concatenate(returned, axis=1) if CHUNKS > 1 else returned[0]
+    back = back.reshape(half, ser_local, total)
+    block = 16
+    keep, give = pl.pallas_call(
+        join_kernel,
+        grid=(half // block,),
+        in_specs=[
+            pl.BlockSpec((block, ser_local, total), lambda i: (i, 0, 0)),
+            pl.BlockSpec((ser_local, block, width), lambda i: (0, i, 0)),
+            pl.BlockSpec((ser_local, block, width), lambda i: (0, i, 0)),
+            pl.BlockSpec((total, total), lambda i: (0, 0)),
+        ],
+        out_specs=[pl.BlockSpec((ser_local, block, width), lambda i: (0, i, 0))] * 2,
+        out_shape=[jax.ShapeDtypeStruct((ser_local, half, width), jnp.bfloat16)] * 2,
+        compiler_params=params(),
+        name="join_path",
+    )(back, time_own, time_other, w_full)
+    taken = lax.ppermute(give, "mp", swap)
+    is_low = me == 0
+    return jnp.concatenate(
+        [jnp.where(is_low, keep, taken), jnp.where(is_low, taken, keep)], axis=1
+    )
 
 
 def time_attend(time_qkv):
@@ -41,7 +231,7 @@
     ).astype(jnp.bfloat16)
 
 
-def per_device(series_in, norm_gain, w_time, w_group, w_gate, w_out, group_of):
+def split_heads(series_in, norm_gain, w_time, w_group, w_gate, w_out, group_of):
     ser_local, patches, width = series_in.shape
     heads_local = w_time.shape[1]
     head_size = w_time.shape[2] // 3
@@ -77,6 +267,16 @@
         ser_local, patches, width
     )
     return lax.psum_scatter(head_term.astype(jnp.bfloat16), "mp", scatter_dimension=2, tiled=True)
+
+
+def per_device(series_in, norm_gain, w_time, *rest):
+    ser_local, patches, _ = series_in.shape
+    ns, nm = lax.axis_size("series"), lax.axis_size("mp")
+    pairs = w_time.shape[1] % 2 == 0 and (2 * w_time.shape[2] // 3) % 128 == 0
+    tiled = ser_local % 16 == 0 and patches % (ns * nm * CHUNKS) == 0 and patches // nm % 16 == 0
+    if nm == 2 and pairs and tiled:
+        return split_patches(series_in, norm_gain, w_time, *rest)
+    return split_heads(series_in, norm_gain, w_time, *rest)
 
 
 def solution(mesh):

time: 564 us -> 270 us (0.48); the launches traced: 556 us -> 269 us
  local copies, waits for them, and re-layouts: 195 us -> 25.4 us
  matrix products: 108 us -> 0 us
  blocking collectives: 77.4 us -> 0 us
  Pallas kernels: 0 us -> 57.6 us
  waiting for transfers between devices: 113 us -> 148 us
  other arithmetic: 42.5 us -> 10.6 us
  starting transfers between devices: 5.69 us -> 14.4 us
    dot_general x22 -> x0, matrix products: 96.8 us -> none  [the longest x16 25.6 us: group_patch(): jnp.einsum('hij,jhd->ihd', weights, values_in, preferred_element_type=jnp...]
    unnamed x29 -> x9, local copies, waits for them, and re-layouts: 87.1 us -> 2.98 us
    unnamed x3 -> x2, waiting for transfers between devices: 77.7 us -> 0.03 us
    all_to_all x1 -> x0, blocking collectives: 77.4 us -> none  [per_device(): lax.all_to_all(own_columns, 'series', split_axis=1, concat_axis=0, tiled=...]
    all_gather x1 -> x2, waiting for transfers between devices: 35.1 us -> 100 us  [the longest x1 63.2 us: split_patches(): w_mix = lax.all_gather(w_mix, 'mp', axis=0)]
    pallas_call x0 -> x3, Pallas kernels: none -> 57.6 us  [the longest x1 24.4 us: split_patches(): pl.pallas_call(partial(time_kernel, head_size=head_size), grid=(ser_local...]
    ppermute x0 -> x2, waiting for transfers between devices: none -> 47.7 us  [the longest x1 35.5 us: split_patches(): taken = lax.ppermute(give, 'mp', swap)]
    another operation x1 -> x0, local copies, waits for them, and re-layouts: 45.5 us -> none  [per_device(): owned = owned.reshape(all_series, patch_local, heads_local, 3, head_size)]
  transfers between devices with their start and end apart: 3 -> 6, of which waited for: 2 -> 4; matrix products, arithmetic and copies ran while one was open for 23% -> 8% of each run, Pallas kernels for 0% -> 9%
where the time goes in v1:
time: 270 us; the launch traced here: 269 us
  waiting for transfers between devices  148 us (55%)
  Pallas kernels  57.6 us (21%)
  local copies, waits for them, and re-layouts  25.4 us (9%)
  starting transfers between devices  14.4 us (5%)
  between operations  13.5 us (5%)
  other arithmetic  10.6 us (4%)
    all_gather x1, waiting for transfers between devices, split_patches(): w_mix = lax.all_gather(w_mix, 'mp', axis=0)  63.2 us
    all_gather x1, waiting for transfers between devices, split_patches(): w_full = lax.all_gather(w_out, 'mp', axis=0, tiled=True)  37 us
    ppermute x1, waiting for transfers between devices, split_patches(): taken = lax.ppermute(give, 'mp', swap)  35.5 us
    pallas_call x1, Pallas kernels, split_patches(): pl.pallas_call(partial(time_kernel, head_size=head_size), grid=(ser_local...  24.4 us
    pallas_call x1, Pallas kernels, split_patches(): pl.pallas_call(partial(group_kernel, head_size=head_size), grid=(step,),...  23.5 us
    ppermute x1, waiting for transfers between devices, split_patches(): time_other = lax.ppermute(time_send, 'mp', swap)  12.1 us
    pallas_call x1, Pallas kernels, split_patches(): pl.pallas_call(join_kernel, grid=(half // block,), in_specs=[pl.BlockSpec...  9.78 us
    all_to_all x1, starting transfers between devices, split_patches(): lax.all_to_all(piece, 'series', split_axis=0, concat_axis=0, tiled=True)  7.59 us
  transfers between devices with their start and end apart: 6, of which 4 were waited for; matrix products, arithmetic and copies ran while one was open for 8% of the time, Pallas kernels for 9%

profile of v1, /device:TPU:0, one launch (start us, length us, event | category | flops | bytes accessed | tf_op | source)
XLA Modules:
  0.0 269.4 jit_solution(7445796845335569439)
XLA Ops:
  6.5 2.6 fusion
  9.2 2.7 fusion.2
  11.8 3.4 %copy.16 = bf16[16,128,768]{2,0,1:T(8,128)(2,1)} copy(bf16[16,128,768]{2,1,0:T(8,128)(2,1)S(1)} %fusion.2) | data formatting | bytes 6291456 | tf_op jit(solution)/shard_map/convert_element_type | solution.py:17
  15.3 7.6 %all-to-all-start = ((bf16[16,8,16,768]{3,2,1,0:T(8,128)(2,1)}), bf16[16,8,16,768]{3,2,1,0:T(8,128)(2,1)}, u32[]{:S(2)}, u32[]{:S(2)}) async-start(bf16[16,8,16,768]{3,2,1,0:T(8,128)(2,1)} %bitcast.1), calls=%async_computation | async-start | bytes 6291456 | tf_op jit(solution)/shard_map/all_to_all | solution.py:130
  23.1 1.3 copy.18
  24.4 1.6 pad_maximum_fusion.1
  26.0 0.8 copy.20.row_ref
  26.8 63.2 %all-gather.6.cloned.1.call-done = bf16[1536,1536]{0,1:T(8,128)(2,1)} async-done(((bf16[768,1536]{0,1:T(8,128)(2,1)}), bf16[1536,1536]{0,1:T(8,128)(2,1)}) %all-gather.6.cloned.1.call-update) | async-done | bytes 4718608 | tf_op jit(solution)/shard_map/all_gather | solution.py:123
  90.1 6.7 %copy.19 = bf16[1536,1536]{1,0:T(8,128)(2,1)} copy(bf16[1536,1536]{0,1:T(8,128)(2,1)} %all-gather.6.cloned.1.call-done) | data formatting | bytes 9437184 | tf_op jit(solution)/shard_map/all_gather | solution.py:123
  96.8 23.5 %group_path.1 = bf16[16,8,16,768]{3,2,1,0:T(8,128)(2,1)} custom-call(bf16[16,8,16,768]{3,2,1,0:T(8,128)(2,1)} %all-to-all-done.x_ref, bf16[2,768,1536]{2,1,0:T(8,128)(2,1)} %bitcast.18, s32[256,1]{1,0:T(8,128)} %copy.20.row_ref, s32[1,256]{1,0:T(1,128)} %bitcast.21), custom_call_target="tpu_custom_call" | custom-call | flops 12884901888 | bytes 6291456 | tf_op jit(solution)/shard_map/group_path/pallas_call | solution.py:158
  120.2 5.6 %all-to-all-start.1 = ((bf16[16,8,16,768]{3,2,1,0:T(8,128)(2,1)}), bf16[16,8,16,768]{3,2,1,0:T(8,128)(2,1)S(1)}, u32[]{:S(2)}, u32[]{:S(2)}) async-start(bf16[16,8,16,768]{3,2,1,0:T(8,128)(2,1)} %group_path.1), calls=%async_computation.1 | async-start | bytes 6291456 | tf_op jit(solution)/shard_map/all_to_all | solution.py:178
  125.9 0.6 reshape.42.gain_ref
  126.5 2.9 %copy.21 = bf16[768,3,6,64]{0,3,2,1:T(8,128)(2,1)} copy(bf16[768,3,6,64]{0,3,1,2:T(8,128)(2,1)} %bitcast.20) | data formatting | bytes 3538944 | tf_op jit(solution)/shard_map/transpose | solution.py:102
  129.4 3.9 %copy.22.w_ref = bf16[768,1152]{1,0:T(8,128)(2,1)} copy(bf16[768,1152]{0,1:T(8,128)(2,1)} %bitcast.17) | data formatting | bytes 3538944 | tf_op jit(solution)/shard_map/reshape | solution.py:102
  133.2 24.4 %time_path.1 = bf16[16,256,384]{2,1,0:T(8,128)(2,1)} custom-call(bf16[16,256,768]{2,1,0:T(8,128)(2,1)} %x_ref.1, f32[1,768]{1,0:T(1,128)} %reshape.42.gain_ref, bf16[768,1152]{1,0:T(8,128)(2,1)} %copy.22.w_ref), custom_call_target="tpu_custom_call" | custom-call | flops 10468982784 | bytes 9437184 | tf_op jit(solution)/shard_map/time_path/pallas_call | solution.py:132
  157.6 4.1 %constant_dynamic-slice_fusion = (bf16[16,128,384]{2,1,0:T(8,128)(2,1)}, bf16[16,128,384]{2,1,0:T(8,128)(2,1)}) fusion(bf16[16,256,384]{2,1,0:T(8,128)(2,1)} %time_path.1, s32[]{:T(128)S(6)} %select_n.21, s32[]{:T(128)S(6)} %select_n.20), kind=kLoop, calls=%fused_computation.10 | loop fusion | bytes 6291464 | tf_op jit(solution)/shard_map/dynamic_slice | solution.py:152
  161.7 0.5 collective-permute-start
  162.2 37.0 %all-gather.4.cloned.1.call-done.w_ref = bf16[768,768]{1,0:T(8,128)(2,1)} async-done(((bf16[384,768]{1,0:T(8,128)(2,1)}), bf16[768,768]{1,0:T(8,128)(2,1)}) %all-gather.4.cloned.1.call-update) | async-done | bytes 1179664 | tf_op jit(solution)/shard_map/all_gather | solution.py:124
  199.2 12.1 %collective-permute-done.other_ref = bf16[16,128,384]{2,1,0:T(8,128)(2,1)} collective-permute-done((bf16[16,128,384]{2,1,0:T(8,128)(2,1)}, bf16[16,128,384]{2,1,0:T(8,128)(2,1)}, u32[]{:S(2)}, u32[]{:S(2)}) %collective-permute-start) | collective-permute-done | bytes 1572896 | tf_op jit(solution)/shard_map/ppermute | solution.py:153
  211.3 1.7 copy-done
  213.0 9.8 %join_path.1 = (bf16[16,128,384]{2,1,0:T(8,128)(2,1)}, bf16[16,128,384]{2,1,0:T(8,128)(2,1)}) custom-call(bf16[128,16,768]{2,1,0:T(8,128)(2,1)} %bitcast.15, bf16[16,128,384]{2,1,0:T(8,128)(2,1)} %get-tuple-element.12.own_ref, bf16[16,128,384]{2,1,0:T(8,128)(2,1)} %collective-permute-done.other_ref, bf16[768,768]{1,0:T(8,128)(2,1)} %all-gather.4.cloned.1.call-done.w_ref), custom_call_target="tpu_custom_call" | custom-call | tf_op jit(solution)/shard_map/join_path/pallas_call | solution.py:184
  223.3 35.5 %collective-permute-done.1 = bf16[16,128,384]{2,1,0:T(8,128)(2,1)S(1)} collective-permute-done((bf16[16,128,384]{2,1,0:T(8,128)(2,1)}, bf16[16,128,384]{2,1,0:T(8,128)(2,1)S(1)}, u32[]{:S(2)}, u32[]{:S(2)}) %collective-permute-start.1) | collective-permute-done | bytes 1572896 | tf_op jit(solution)/shard_map/ppermute | solution.py:198
  258.9 1.7 broadcast_select_fusion.1
  260.6 2.0 pad_maximum_fusion
  (16 shorter events, 0.8 us)
Async XLA Ops:
  6.5 2.6 copy-start.2
  15.3 7.7 %copy-start.1 = (bf16[768,6,192]{0,2,1:T(8,128)(2,1)S(1)}, bf16[768,6,192]{0,2,1:T(8,128)(2,1)}, u32[]{:S(2)}) copy-start(bf16[768,6,192]{0,2,1:T(8,128)(2,1)} %param.10) | copy-start | bytes 5308420
  15.3 81.5 %all-to-all-start = ((bf16[16,8,16,768]{3,2,1,0:T(8,128)(2,1)}), bf16[16,8,16,768]{3,2,1,0:T(8,128)(2,1)}, u32[]{:S(2)}, u32[]{:S(2)}) async-start(bf16[16,8,16,768]{3,2,1,0:T(8,128)(2,1)} %bitcast.1), calls=%async_computation | async-start | bytes 6291456 | tf_op jit(solution)/shard_map/all_to_all | solution.py:130
  22.9 67.2 %all-gather.6.cloned.1.call-start = ((), (), s32[]{:S(2)}) async-start(), calls=%async_computation.3 | async-start | bytes 7077888 | tf_op jit(solution)/shard_map/all_gather | solution.py:123
  24.4 1.6 copy-start.3
  120.2 91.1 %all-to-all-start.1 = ((bf16[16,8,16,768]{3,2,1,0:T(8,128)(2,1)}), bf16[16,8,16,768]{3,2,1,0:T(8,128)(2,1)S(1)}, u32[]{:S(2)}, u32[]{:S(2)}) async-start(bf16[16,8,16,768]{3,2,1,0:T(8,128)(2,1)} %group_path.1), calls=%async_computation.1 | async-start | bytes 6291456 | tf_op jit(solution)/shard_map/all_to_all | solution.py:178
  125.9 73.3 %all-gather.4.cloned.1.call-start = ((), (), s32[]{:S(2)}) async-start(), calls=%async_computation.2 | async-start | bytes 1769472 | tf_op jit(solution)/shard_map/all_gather | solution.py:124
  161.7 49.7 %collective-permute-start = (bf16[16,128,384]{2,1,0:T(8,128)(2,1)}, bf16[16,128,384]{2,1,0:T(8,128)(2,1)}, u32[]{:S(2)}, u32[]{:S(2)}) collective-permute-start(bf16[16,128,384]{2,1,0:T(8,128)(2,1)} %get-tuple-element.11), channel_id=1, source_target_pairs={{0,1},{1,0},{2,3},{3,2},{4,5},{5,4},{6,7},{7,6},{8,9},{9,8},{10,11... | collective-permute-start | bytes 4718600 | tf_op jit(solution)/shard_map/ppermute | solution.py:153
  211.3 1.7 copy-start
  222.8 36.1 %collective-permute-start.1 = (bf16[16,128,384]{2,1,0:T(8,128)(2,1)}, bf16[16,128,384]{2,1,0:T(8,128)(2,1)S(1)}, u32[]{:S(2)}, u32[]{:S(2)}) collective-permute-start(bf16[16,128,384]{2,1,0:T(8,128)(2,1)} %get-tuple-element.8), channel_id=1, source_target_pairs={{0,1},{1,0},{2,3},{3,2},{4,5},{5,4},{6,7},{7,6},{8,9},{9,8},{10,11... | collective-permute-start | bytes 4718600 | tf_op jit(solution)/shard_map/ppermute | solution.py:198
Sparse Core Ops, SparseCore 0:
  26.1 63.8 all-gather.5
  162.4 36.7 all-gather.3

commit v2 on v1

--- a/solution.py
+++ b/solution.py
@@ -7,7 +7,8 @@
 from jax.experimental.pallas import tpu as pltpu
 from jax.sharding import PartitionSpec as P
 
-CHUNKS = 1
+
+CHUNKS = 2
 VMEM_BYTES = 60 * 1024 * 1024
 
 
@@ -18,7 +19,6 @@
 
 
 def attend_pair(queries, keys_in, values_in, bias, head_size):
-    rows = queries.shape[0]
     lane = lax.broadcasted_iota(jnp.int32, queries.shape, 1)
     first = lane < head_size
     zero = jnp.zeros_like(queries)
@@ -40,36 +40,85 @@
     return tops / sums
 
 
-def time_kernel(x_ref, gain_ref, w_ref, out_ref, *, head_size):
+def fill_heads(made_ref, at, part, first_head, head_size, width):
+    for head in range(part.shape[0]):
+        for kind in range(3):
+            to = kind * width + (first_head + head) * head_size
+            if not isinstance(to, int):
+                to = pl.multiple_of(to, head_size)
+            rows = part[head, kind * head_size : (kind + 1) * head_size]
+            made_ref[at, pl.ds(to, head_size)] = rows
+
+
+def project(rows, weight):
+    return lax.dot_general(
+        rows, weight, (((1,), (1,)), ((), ())), preferred_element_type=jnp.float32
+    )
+
+
+def prep_kernel(_, x_ref, gain_ref, *rest):
+    out_ref = rest[-1]
+    normed = rms_norm(x_ref[...], gain_ref[...].reshape(1, 1, -1)).astype(jnp.float32)
+    out_ref[...] = jnp.swapaxes(normed, 0, 1).astype(jnp.bfloat16)
+
+
+def time_kernel(x_ref, gain_ref, w_ref, _, own_ref, give_ref, made_ref, *, head_size):
+    is_low = lax.axis_index("mp") == 0
+    width = own_ref.shape[-1]
+    half = own_ref.shape[1]
+
+    @pl.when(pl.program_id(0) == 0)
+    def _():
+        fill_heads(made_ref, 0, w_ref, 0, head_size, width)
+
     normed = rms_norm(x_ref[0], gain_ref[...])
-    width = out_ref.shape[-1]
     pair = 2 * head_size
     scale = head_size ** (-0.5)
-    qkv = jnp.dot(normed, w_ref[...], preferred_element_type=jnp.float32)
+    qkv = project(normed, made_ref[0])
     queries = (qkv[:, :width].astype(jnp.bfloat16) * scale).astype(jnp.bfloat16)
     keys_in = qkv[:, width : 2 * width].astype(jnp.bfloat16)
     values_in = qkv[:, 2 * width :].astype(jnp.bfloat16)
     for at in range(0, width, pair):
         cut = slice(at, at + pair)
-        out_ref[0, :, cut] = attend_pair(
+        got = attend_pair(
             queries[:, cut], keys_in[:, cut], values_in[:, cut], None, head_size
-        ).astype(jnp.bfloat16)
-
-
-def group_kernel(x_ref, w_ref, row_ref, col_ref, out_ref, *, head_size):
+        )
+        low, high = got[:half], got[half:]
+        own_ref[0, :, cut] = jnp.where(is_low, low, high).astype(jnp.bfloat16)
+        give_ref[0, :, cut] = jnp.where(is_low, high, low).astype(jnp.bfloat16)
+
+
+def group_kernel(
+    x_ref, w_ref, wa_ref, wb_ref, g_ref, ga_ref, gb_ref, row_ref, col_ref, _, out_ref,
+    made_ref, gate_ref, *, head_size
+):
+    me = lax.axis_index("mp")
+    core = lax.axis_index("series") % 2
     sources, _, ser_local, depth = x_ref.shape
-    members = w_ref.shape[0]
-    width = w_ref.shape[2] // 4
+    width = g_ref.shape[1]
+    half_heads = wa_ref.shape[0]
+    half_depth = ga_ref.shape[0]
+
+    @pl.when(pl.program_id(0) == 0)
+    def _():
+        fill_heads(made_ref, me, w_ref, 0, head_size, width)
+        fill_heads(made_ref, 1 - me, wa_ref, core * half_heads, head_size, width)
+        fill_heads(made_ref, 1 - me, wb_ref, (1 - core) * half_heads, head_size, width)
+        gate_ref[me] = g_ref[...]
+        for part, at in ((ga_ref, core), (gb_ref, 1 - core)):
+            to = pl.multiple_of(at * half_depth, half_depth)
+            gate_ref[1 - me, pl.ds(to, half_depth)] = part[...]
+
     pair = 2 * head_size
     scale = head_size ** (-0.5)
     rows = x_ref[...].reshape(sources * ser_local, depth)
     bias = jnp.where(row_ref[...] == col_ref[...], 0.0, -1e30).astype(jnp.float32)
-    for member in range(members):
-        made = jnp.dot(rows, w_ref[member], preferred_element_type=jnp.float32)
+    for member in range(2):
+        made = project(rows, made_ref[member])
         queries = (made[:, :width].astype(jnp.bfloat16) * scale).astype(jnp.bfloat16)
         keys_in = made[:, width : 2 * width].astype(jnp.bfloat16)
-        values_in = made[:, 2 * width : 3 * width].astype(jnp.bfloat16)
-        gate = jax.nn.sigmoid(made[:, 3 * width :])
+        values_in = made[:, 2 * width :].astype(jnp.bfloat16)
+        gate = jax.nn.sigmoid(jnp.dot(rows, gate_ref[member], preferred_element_type=jnp.float32))
         for at in range(0, width, pair):
             cut = slice(at, at + pair)
             got = attend_pair(queries[:, cut], keys_in[:, cut], values_in[:, cut], bias, head_size)
@@ -78,10 +127,20 @@
             out_ref[:, 0, :, to : to + pair] = got.reshape(sources, ser_local, pair)
 
 
-def join_kernel(group_ref, own_ref, other_ref, w_ref, keep_ref, send_ref):
+def join_kernel(group_ref, own_ref, other_ref, w_ref, wa_ref, wb_ref, keep_ref, send_ref, full_ref):
     me = lax.axis_index("mp")
+    core = lax.axis_index("series") % 2
     block, ser_local, width = group_ref.shape
     half = width // 2
+    quarter = half // 2
+
+    @pl.when(pl.program_id(0) == 0)
+    def _():
+        full_ref[pl.ds(pl.multiple_of(me * half, half), half)] = w_ref[...]
+        for part, at in ((wa_ref, core), (wb_ref, 1 - core)):
+            to = pl.multiple_of((1 - me) * half + at * quarter, quarter)
+            full_ref[pl.ds(to, quarter)] = part[...]
+
     group = jnp.swapaxes(group_ref[...].astype(jnp.float32), 0, 1).reshape(ser_local * block, width)
     own = own_ref[...].reshape(ser_local * block, half).astype(jnp.float32)
     other = other_ref[...].reshape(ser_local * block, half).astype(jnp.float32)
@@ -89,17 +148,11 @@
     low = jnp.where(is_low, own, other)
     high = jnp.where(is_low, other, own)
     merged = (jnp.concatenate([low, high], axis=1) + group).astype(jnp.bfloat16)
-    result = jnp.dot(merged, w_ref[...], preferred_element_type=jnp.float32).astype(jnp.bfloat16)
+    result = jnp.dot(merged, full_ref[...], preferred_element_type=jnp.float32).astype(jnp.bfloat16)
     result = result.reshape(ser_local, block, width)
     low, high = result[:, :, :half], result[:, :, half:]
     keep_ref[...] = jnp.where(is_low, low, high)
     send_ref[...] = jnp.where(is_low, high, low)
-
-
-def join_heads(weight):
-    depth, heads, triple = weight.shape
-    split = weight.reshape(depth, heads, 3, triple // 3)
-    return jnp.swapaxes(split, 1, 2).reshape(depth, heads * triple)
 
 
 def split_patches(series_in, norm_gain, w_time, w_group, w_gate, w_out, group_of):
@@ -107,38 +160,80 @@
     heads_local = w_time.shape[1]
     head_size = w_time.shape[2] // 3
     width = heads_local * head_size
-    total = heads_local * head_size * 2
     ns, nm = lax.axis_size("series"), lax.axis_size("mp")
+    total = width * nm
     me = lax.axis_index("mp")
+    core = lax.axis_index("series") % 2
     half = patches // nm
     each = half // ns
     n_series = group_of.shape[0]
     params = lambda: pltpu.CompilerParams(vmem_limit_bytes=VMEM_BYTES)
-
-    own_half = lax.dynamic_slice_in_dim(series_in, me * half, half, 1)
-    send = rms_norm(own_half, norm_gain)
-    send = jnp.transpose(send.reshape(ser_local, ns, each, depth), (1, 2, 0, 3))
-
-    w_mix = jnp.concatenate([join_heads(w_group), w_gate], axis=1)
-    w_mix = lax.all_gather(w_mix, "mp", axis=0)
-    w_full = lax.all_gather(w_out, "mp", axis=0, tiled=True)
+    whole = lambda *shape: pl.BlockSpec(shape, lambda *i: (0,) * len(shape))
+    unread = pl.BlockSpec(memory_space=pl.ANY)
+    swap = [(i, nm - 1 - i) for i in range(nm)]
+    sibling = [(i, i ^ 1) for i in range(ns)]
+
+    def from_partner(weight):
+        rows = weight.shape[0] // 2
+        part = lax.dynamic_slice_in_dim(weight, core * rows, rows, 0)
+        first = lax.ppermute(part, "mp", swap)
+        return first, lax.ppermute(first, "series", sibling)
 
     step = each // CHUNKS
-    received = []
-    for c in range(CHUNKS):
-        piece = send[:, c * step : (c + 1) * step]
-        received.append(lax.all_to_all(piece, "series", split_axis=0, concat_axis=0, tiled=True))
-
-    time_out = pl.pallas_call(
+    block = 16
+    gain = norm_gain.reshape(1, depth)
+    me_ref = me.astype(jnp.int32).reshape(1)
+    sent, received = [], []
+    chunk = ns * step
+
+    def send_chunk(c, after):
+        piece = pl.pallas_call(
+            prep_kernel,
+            grid_spec=pltpu.PrefetchScalarGridSpec(
+                num_scalar_prefetch=1,
+                grid=(chunk // block,),
+                in_specs=[
+                    pl.BlockSpec(
+                        (ser_local, block, depth),
+                        lambda i, m, c=c: (0, (m[0] * half + c * chunk) // block + i, 0),
+                    ),
+                    whole(1, depth),
+                    *[unread] * len(after),
+                ],
+                out_specs=pl.BlockSpec((block, ser_local, depth), lambda i, m: (i, 0, 0)),
+            ),
+            out_shape=jax.ShapeDtypeStruct((chunk, ser_local, depth), jnp.bfloat16),
+            compiler_params=params(),
+            name="prep_path",
+        )(me_ref, series_in, gain, *after)
+        sent.append(piece)
+        received.append(
+            lax.all_to_all(
+                piece.reshape(ns, step, ser_local, depth),
+                "series", split_axis=0, concat_axis=0, tiled=True,
+            )
+        )
+
+    send_chunk(0, ())
+
+    turned = lambda weight: jnp.transpose(weight, (1, 2, 0))
+    group_own = turned(w_group)
+    group_a, group_b = from_partner(group_own)
+    gate_a, gate_b = from_partner(w_gate)
+    out_a, out_b = from_partner(w_out)
+
+    time_own, time_give = pl.pallas_call(
         partial(time_kernel, head_size=head_size),
         grid=(ser_local,),
         in_specs=[
             pl.BlockSpec((1, patches, depth), lambda i: (i, 0, 0)),
-            pl.BlockSpec((1, depth), lambda i: (0, 0)),
-            pl.BlockSpec((depth, 3 * width), lambda i: (0, 0)),
+            whole(1, depth),
+            whole(heads_local, 3 * head_size, depth),
+            unread,
         ],
-        out_specs=pl.BlockSpec((1, patches, width), lambda i: (i, 0, 0)),
-        out_shape=jax.ShapeDtypeStruct((ser_local, patches, width), jnp.bfloat16),
+        out_specs=[pl.BlockSpec((1, half, width), lambda i: (i, 0, 0))] * 2,
+        out_shape=[jax.ShapeDtypeStruct((ser_local, half, width), jnp.bfloat16)] * 2,
+        scratch_shapes=[pltpu.VMEM((1, 3 * width, depth), jnp.bfloat16)],
         compiler_params=params(),
         name="time_path",
         cost_estimate=pl.CostEstimate(
@@ -146,26 +241,37 @@
             bytes_accessed=ser_local * patches * (depth + width) * 2,
             transcendentals=ser_local * heads_local * patches * patches,
         ),
-    )(series_in, norm_gain.reshape(1, depth), join_heads(w_time))
-
-    swap = [(i, nm - 1 - i) for i in range(nm)]
-    time_send = lax.dynamic_slice_in_dim(time_out, (nm - 1 - me) * half, half, 1)
-    time_other = lax.ppermute(time_send, "mp", swap)
-    time_own = lax.dynamic_slice_in_dim(time_out, me * half, half, 1)
-
-    returned = []
+    )(series_in, gain, turned(w_time), sent[0])
+    for c in range(1, CHUNKS):
+        send_chunk(c, (time_own, group_a, gate_a, out_a) if c == 1 else (sent[-1],))
+
+    time_other = lax.ppermute(time_give, "mp", swap)
+
+    out = jnp.zeros((ser_local, patches, width), jnp.bfloat16)
+    last = time_own
+    backs = []
     for c in range(CHUNKS):
-        group_out = pl.pallas_call(
+        call = pl.pallas_call(
             partial(group_kernel, head_size=head_size),
             grid=(step,),
             in_specs=[
                 pl.BlockSpec((ns, 1, ser_local, depth), lambda i: (0, i, 0, 0)),
-                pl.BlockSpec((nm, depth, 4 * width), lambda i: (0, 0, 0)),
-                pl.BlockSpec((n_series, 1), lambda i: (0, 0)),
-                pl.BlockSpec((1, n_series), lambda i: (0, 0)),
+                whole(*group_own.shape),
+                whole(*group_a.shape),
+                whole(*group_b.shape),
+                whole(*w_gate.shape),
+                whole(*gate_a.shape),
+                whole(*gate_b.shape),
+                whole(n_series, 1),
+                whole(1, n_series),
+                unread,
             ],
             out_specs=pl.BlockSpec((ns, 1, ser_local, total), lambda i: (0, i, 0, 0)),
             out_shape=jax.ShapeDtypeStruct((ns, step, ser_local, total), jnp.bfloat16),
+            scratch_shapes=[
+                pltpu.VMEM((nm, 3 * width, depth), jnp.bfloat16),
+                pltpu.VMEM((nm, depth, width), jnp.bfloat16),
+            ],
             compiler_params=params(),
             name="group_path",
             cost_estimate=pl.CostEstimate(
@@ -173,33 +279,45 @@
                 bytes_accessed=step * n_series * (depth + total) * 2,
                 transcendentals=step * nm * heads_local * n_series * n_series,
             ),
-        )(received[c], w_mix, group_of.reshape(n_series, 1), group_of.reshape(1, n_series))
-        returned.append(
+        )
+        group_out = call(
+        received[c], group_own, group_a, group_b, w_gate, gate_a, gate_b,
+        group_of.reshape(n_series, 1), group_of.reshape(1, n_series), last,
+        )
+        last = group_out
+        backs.append(
             lax.all_to_all(group_out, "series", split_axis=0, concat_axis=0, tiled=True)
         )
 
-    back = jnp.concatenate(returned, axis=1) if CHUNKS > 1 else returned[0]
-    back = back.reshape(half, ser_local, total)
-    block = 16
-    keep, give = pl.pallas_call(
-        join_kernel,
-        grid=(half // block,),
-        in_specs=[
-            pl.BlockSpec((block, ser_local, total), lambda i: (i, 0, 0)),
-            pl.BlockSpec((ser_local, block, width), lambda i: (0, i, 0)),
-            pl.BlockSpec((ser_local, block, width), lambda i: (0, i, 0)),
-            pl.BlockSpec((total, total), lambda i: (0, 0)),
-        ],
-        out_specs=[pl.BlockSpec((ser_local, block, width), lambda i: (0, i, 0))] * 2,
-        out_shape=[jax.ShapeDtypeStruct((ser_local, half, width), jnp.bfloat16)] * 2,
-        compiler_params=params(),
-        name="join_path",
-    )(back, time_own, time_other, w_full)
-    taken = lax.ppermute(give, "mp", swap)
-    is_low = me == 0
-    return jnp.concatenate(
-        [jnp.where(is_low, keep, taken), jnp.where(is_low, taken, keep)], axis=1
-    )
+    for c in range(CHUNKS):
+        back = backs[c].reshape(chunk, ser_local, total)
+        at_chunk = lambda i, c=c: (0, c * chunk // block + i, 0)
+        keep, give = pl.pallas_call(
+            join_kernel,
+            grid=(chunk // block,),
+            in_specs=[
+                pl.BlockSpec((block, ser_local, total), lambda i: (i, 0, 0)),
+                pl.BlockSpec((ser_local, block, width), at_chunk),
+                pl.BlockSpec((ser_local, block, width), at_chunk),
+                whole(*w_out.shape),
+                whole(*out_a.shape),
+                whole(*out_b.shape),
+            ],
+            out_specs=[pl.BlockSpec((ser_local, block, width), lambda i: (0, i, 0))] * 2,
+            out_shape=[jax.ShapeDtypeStruct((ser_local, chunk, width), jnp.bfloat16)] * 2,
+            scratch_shapes=[pltpu.VMEM((total, total), jnp.bfloat16)],
+            compiler_params=params(),
+            name="join_path",
+            cost_estimate=pl.CostEstimate(
+                flops=2 * chunk * ser_local * total * total,
+                bytes_accessed=4 * chunk * ser_local * total * 2,
+                transcendentals=0,
+            ),
+        )(back, time_own, time_other, w_out, out_a, out_b)
+        taken = lax.ppermute(give, "mp", swap)
+        out = lax.dynamic_update_slice_in_dim(out, keep, me * half + c * chunk, 1)
+        out = lax.dynamic_update_slice_in_dim(out, taken, (nm - 1 - me) * half + c * chunk, 1)
+    return out
 
 
 def time_attend(time_qkv):
@@ -272,8 +390,9 @@
 def per_device(series_in, norm_gain, w_time, *rest):
     ser_local, patches, _ = series_in.shape
     ns, nm = lax.axis_size("series"), lax.axis_size("mp")
-    pairs = w_time.shape[1] % 2 == 0 and (2 * w_time.shape[2] // 3) % 128 == 0
-    tiled = ser_local % 16 == 0 and patches % (ns * nm * CHUNKS) == 0 and patches // nm % 16 == 0
+    pairs = w_time.shape[1] % 2 == 0 and w_time.shape[2] % 48 == 0 and (2 * w_time.shape[2] // 3) % 128 == 0
+    tiled = ser_local % 16 == 0 and patches % (ns * nm * CHUNKS) == 0 and patches // nm % (16 * CHUNKS) == 0
+    tiled = tiled and ns % 2 == 0 and w_time.shape[0] % 32 == 0
     if nm == 2 and pairs and tiled:
         return split_patches(series_in, norm_gain, w_time, *rest)
     return split_heads(series_in, norm_gain, w_time, *rest)

time: 270 us -> 224 us (0.83)
  waiting for transfers between devices: 148 us -> 94.7 us
  starting transfers between devices: 14.4 us -> 39.4 us
  Pallas kernels: 57.6 us -> 78.2 us
  local copies, waits for them, and re-layouts: 25.4 us -> 10.7 us
  between operations: 13.5 us -> 0.16 us
  other arithmetic: 10.6 us -> 0 us
    all_gather x2 -> x0, waiting for transfers between devices: 100 us -> none  [the longest x1 63.2 us: split_patches(): w_mix = lax.all_gather(w_mix, 'mp', axis=0)]
    ppermute x1 -> x7, waiting for transfers between devices: 12.1 us -> 38.9 us  [the longest x1 33.9 us: split_patches(): time_other = lax.ppermute(time_give, 'mp', swap)]
    pallas_call x2 -> x6, Pallas kernels: 33.2 us -> 50.9 us  [the longest x2 30.5 us: split_patches(): call(received[c], group_own, group_a, group_b, w_gate, gate_a, gate_b, gr...]
    all_to_all x1 -> x2, waiting for transfers between devices: 0.01 us -> 16.6 us  [split_patches(): lax.all_to_all(group_out, 'series', split_axis=0, concat_axis=0, tiled=True)]
    all_to_all x1 -> x2, waiting for transfers between devices: 0.01 us -> 13.3 us  [send_chunk(): lax.all_to_all(piece.reshape(ns, step, ser_local, depth), 'series', split...]
    all_to_all x1 -> x2, starting transfers between devices: 5.62 us -> 18.2 us  [split_patches(): lax.all_to_all(group_out, 'series', split_axis=0, concat_axis=0, tiled=True)]
    ppermute x1 -> x2, waiting for transfers between devices: 35.5 us -> 25.9 us  [split_patches(): taken = lax.ppermute(give, 'mp', swap)]
    all_gather x1 -> x0, local copies, waits for them, and re-layouts: 6.72 us -> none  [split_patches(): w_mix = lax.all_gather(w_mix, 'mp', axis=0)]
  transfers between devices with their start and end apart: 6 -> 13, of which waited for: 4 -> 8; matrix products, arithmetic and copies ran while one was open for 8% -> 3% of each run, Pallas kernels for 9% -> 33%
where the time goes in v2:
time: 224 us; the launch traced here: 223 us
  waiting for transfers between devices  94.7 us (42%)
  Pallas kernels  78.2 us (35%)
  starting transfers between devices  39.4 us (18%)
  local copies, waits for them, and re-layouts  10.7 us (5%)
    ppermute x1, waiting for transfers between devices, split_patches(): time_other = lax.ppermute(time_give, 'mp', swap)  33.9 us
    pallas_call x2, Pallas kernels, split_patches(): call(received[c], group_own, group_a, group_b, w_gate, gate_a, gate_b, gr...  30.5 us
    pallas_call x1, Pallas kernels, split_patches(): pl.pallas_call(partial(time_kernel, head_size=head_size), grid=(ser_local...  27.2 us
    ppermute x2, waiting for transfers between devices, split_patches(): taken = lax.ppermute(give, 'mp', swap)  25.9 us
    all_to_all x2, starting transfers between devices, split_patches(): lax.all_to_all(group_out, 'series', split_axis=0, concat_axis=0, tiled=True)  18.2 us
    all_to_all x2, waiting for transfers between devices, split_patches(): lax.all_to_all(group_out, 'series', split_axis=0, concat_axis=0, tiled=True)  16.6 us
    all_to_all x2, starting transfers between devices, send_chunk(): lax.all_to_all(piece.reshape(ns, step, ser_local, depth), 'series', split...  13.4 us
    all_to_all x2, waiting for transfers between devices, send_chunk(): lax.all_to_all(piece.reshape(ns, step, ser_local, depth), 'series', split...  13.3 us
  transfers between devices with their start and end apart: 13, of which 8 were waited for; matrix products, arithmetic and copies ran while one was open for 3% of the time, Pallas kernels for 33%

profile of v2, /device:TPU:0, one launch (start us, length us, event | category | flops | bytes accessed | tf_op | source)
XLA Modules:
  0.0 223.1 jit_solution(1582228145621496135)
XLA Ops:
  1.3 4.2 %prep_path.2._ = bf16[64,16,768]{2,1,0:T(8,128)(2,1)} custom-call(s32[1]{0:T(128)} %bitcast._, bf16[16,256,768]{2,1,0:T(8,128)(2,1)} %x_ref.5, f32[1,768]{1,0:T(1,128)} %reshape.27.gain_ref), custom_call_target="tpu_custom_call" | custom-call | tf_op jit(solution)/shard_map/prep_path/pallas_call | solution.py:190
  5.5 7.5 %all-to-all-start = ((bf16[16,4,16,768]{3,2,1,0:T(8,128)(2,1)}), bf16[16,4,16,768]{3,2,1,0:T(8,128)(2,1)S(1)}, u32[]{:S(2)}, u32[]{:S(2)}) async-start(bf16[16,4,16,768]{3,2,1,0:T(8,128)(2,1)} %bitcast.12), calls=%async_computation | async-start | bytes 3145728 | tf_op jit(solution)/shard_map/all_to_all | solution.py:211
  13.1 2.1 dynamic-slice_bitcast_fusion
  15.2 1.5 collective-permute-start
  16.7 1.7 constant_dynamic-slice_fusion.1
  19.7 1.5 collective-permute-start.5
  21.2 27.2 %time_path.1 = (bf16[16,128,384]{2,1,0:T(8,128)(2,1)}, bf16[16,128,384]{2,1,0:T(8,128)(2,1)}) custom-call(bf16[16,256,768]{2,1,0:T(8,128)(2,1)} %x_ref.5, f32[1,768]{1,0:T(1,128)} %reshape.27.gain_ref, bf16[6,192,768]{2,1,0:T(8,128)(2,1)} %bitcast.20, bf16[64,16,768]{2,1,0:T(8,128)(2,1)} %prep_path.2._), custom_call_target="tpu_custom_call" | custom-call | flops 10468982784 | bytes 9437184 | tf_op jit(solution)/shard_map/time_path/pallas_call | solution.py:225
  48.4 1.6 collective-permute-done.5.wa_ref.rest_3_
  51.0 4.3 %prep_path.3 = bf16[64,16,768]{2,1,0:T(8,128)(2,1)} custom-call(s32[1]{0:T(128)} %bitcast._, bf16[16,256,768]{2,1,0:T(8,128)(2,1)} %x_ref.5, f32[1,768]{1,0:T(1,128)} %reshape.27.gain_ref, bf16[16,128,384]{2,1,0:T(8,128)(2,1)} %get-tuple-element.11._.own_ref.rest_0_, bf16[3,192,768]{2,1,0:T(8,128)(2,1)} %copy-done.9, bf16[384,384]{1,0:T(8,128)(2,1)} %copy-done.12, ...), custom_call_target="tpu_custom_call" | custom-call | tf_op jit(solution)/shard_map/prep_path/pallas_call | solution.py:190
  55.3 5.9 %all-to-all-start.2 = ((bf16[16,4,16,768]{3,2,1,0:T(8,128)(2,1)}), bf16[16,4,16,768]{3,2,1,0:T(8,128)(2,1)S(1)}, u32[]{:S(2)}, u32[]{:S(2)}) async-start(bf16[16,4,16,768]{3,2,1,0:T(8,128)(2,1)} %bitcast.11), calls=%async_computation.2 | async-start | bytes 3145728 | tf_op jit(solution)/shard_map/all_to_all | solution.py:211
  62.6 1.9 collective-permute-done.3.gb_ref
  64.5 15.3 %group_path.2._ = bf16[16,4,16,768]{3,2,1,0:T(8,128)(2,1)} custom-call(bf16[16,4,16,768]{3,2,1,0:T(8,128)(2,1)} %copy-done.6, bf16[6,192,768]{2,1,0:T(8,128)(2,1)} %bitcast.15, bf16[3,192,768]{2,1,0:T(8,128)(2,1)} %copy-done.9, bf16[3,192,768]{2,1,0:T(8,128)(2,1)} %collective-permute-done.1.wb_ref, bf16[768,384]{1,0:T(8,128)(2,1)} %g_ref.3, ...), custom_call_target="tpu_custom_call" | custom-call | flops 6442450944 | bytes 3145728 | tf_op jit(solution)/shard_map/group_path/pallas_call | solution.py:283
  79.7 13.3 %all-to-all-done.2.x_ref = bf16[16,4,16,768]{3,2,1,0:T(8,128)(2,1)S(1)} async-done(((bf16[16,4,16,768]{3,2,1,0:T(8,128)(2,1)}), bf16[16,4,16,768]{3,2,1,0:T(8,128)(2,1)S(1)}, u32[]{:S(2)}, u32[]{:S(2)}) %all-to-all-start.2) | async-done | bytes 1572896 | tf_op jit(solution)/shard_map/all_to_all | solution.py:211
  93.0 9.1 %all-to-all-start.1 = ((bf16[16,4,16,768]{3,2,1,0:T(8,128)(2,1)}), bf16[16,4,16,768]{3,2,1,0:T(8,128)(2,1)S(1)}, u32[]{:S(2)}, u32[]{:S(2)}) async-start(bf16[16,4,16,768]{3,2,1,0:T(8,128)(2,1)} %group_path.2._), calls=%async_computation.1 | async-start | bytes 3145728 | tf_op jit(solution)/shard_map/all_to_all | solution.py:289
  102.2 15.3 %group_path.3 = bf16[16,4,16,768]{3,2,1,0:T(8,128)(2,1)} custom-call(bf16[16,4,16,768]{3,2,1,0:T(8,128)(2,1)} %copy-done.7, bf16[6,192,768]{2,1,0:T(8,128)(2,1)} %bitcast.16, bf16[3,192,768]{2,1,0:T(8,128)(2,1)} %copy-done.9, bf16[3,192,768]{2,1,0:T(8,128)(2,1)} %collective-permute-done.1.wb_ref, bf16[768,384]{1,0:T(8,128)(2,1)} %g_ref.3, ...), custom_call_target="tpu_custom_call" | custom-call | flops 6442450944 | bytes 3145728 | tf_op jit(solution)/shard_map/group_path/pallas_call | solution.py:283
  117.4 16.6 %all-to-all-done.1 = bf16[16,4,16,768]{3,2,1,0:T(8,128)(2,1)S(1)} async-done(((bf16[16,4,16,768]{3,2,1,0:T(8,128)(2,1)}), bf16[16,4,16,768]{3,2,1,0:T(8,128)(2,1)S(1)}, u32[]{:S(2)}, u32[]{:S(2)}) %all-to-all-start.1) | async-done | bytes 1572896 | tf_op jit(solution)/shard_map/all_to_all | solution.py:289
  134.0 9.1 %all-to-all-start.3 = ((bf16[16,4,16,768]{3,2,1,0:T(8,128)(2,1)}), bf16[16,4,16,768]{3,2,1,0:T(8,128)(2,1)S(1)}, u32[]{:S(2)}, u32[]{:S(2)}) async-start(bf16[16,4,16,768]{3,2,1,0:T(8,128)(2,1)} %group_path.3), calls=%async_computation.3 | async-start | bytes 3145728 | tf_op jit(solution)/shard_map/all_to_all | solution.py:289
  143.1 1.6 collective-permute-start.4
  146.3 33.9 %collective-permute-done.4.other_ref = bf16[16,128,384]{2,1,0:T(8,128)(2,1)} collective-permute-done((bf16[16,128,384]{2,1,0:T(8,128)(2,1)}, bf16[16,128,384]{2,1,0:T(8,128)(2,1)}, u32[]{:S(2)}, u32[]{:S(2)}) %collective-permute-start.4) | collective-permute-done | bytes 1572896 | tf_op jit(solution)/shard_map/ppermute | solution.py:248
  180.2 5.9 %join_path.2 = (bf16[16,64,384]{2,1,0:T(8,128)(2,1)}, bf16[16,64,384]{2,1,0:T(8,128)(2,1)}) custom-call(bf16[64,16,768]{2,1,0:T(8,128)(2,1)} %bitcast.13, bf16[16,128,384]{2,1,0:T(8,128)(2,1)} %get-tuple-element.11._.own_ref.rest_0_, bf16[16,128,384]{2,1,0:T(8,128)(2,1)} %collective-permute-done.4.other_ref, bf16[384,768]{1,0:T(8,128)(2,1)} %w_ref.3, ...), custom_call_target="tpu_custom_call" | custom-call | flops 1207959552 | bytes 6291456 | tf_op jit(solution)/shard_map/join_path/pallas_call | solution.py:295
  186.1 1.5 collective-permute-start.7
  188.8 6.0 %join_path.3 = (bf16[16,64,384]{2,1,0:T(8,128)(2,1)}, bf16[16,64,384]{2,1,0:T(8,128)(2,1)}) custom-call(bf16[64,16,768]{2,1,0:T(8,128)(2,1)} %bitcast.14, bf16[16,128,384]{2,1,0:T(8,128)(2,1)} %get-tuple-element.11._.own_ref.rest_0_, bf16[16,128,384]{2,1,0:T(8,128)(2,1)} %collective-permute-done.4.other_ref, bf16[384,768]{1,0:T(8,128)(2,1)} %w_ref.3, ...), custom_call_target="tpu_custom_call" | custom-call | flops 1207959552 | bytes 6291456 | tf_op jit(solution)/shard_map/join_path/pallas_call | solution.py:295
  195.9 10.8 %collective-permute-done.7 = bf16[16,64,384]{2,1,0:T(8,128)(2,1)S(1)} collective-permute-done((bf16[16,64,384]{2,1,0:T(8,128)(2,1)}, bf16[16,64,384]{2,1,0:T(8,128)(2,1)S(1)}, u32[]{:S(2)}, u32[]{:S(2)}) %collective-permute-start.7) | collective-permute-done | bytes 786464 | tf_op jit(solution)/shard_map/ppermute | solution.py:317
  207.1 15.1 %collective-permute-done.8 = bf16[16,64,384]{2,1,0:T(8,128)(2,1)S(1)} collective-permute-done((bf16[16,64,384]{2,1,0:T(8,128)(2,1)}, bf16[16,64,384]{2,1,0:T(8,128)(2,1)S(1)}, u32[]{:S(2)}, u32[]{:S(2)}) %collective-permute-start.8) | collective-permute-done | bytes 786464 | tf_op jit(solution)/shard_map/ppermute | solution.py:317
  (49 shorter events, 10.1 us)
Async XLA Ops:
  5.5 13.5 %copy-start.2 = (bf16[384,768]{1,0:T(8,128)(2,1)S(1)}, bf16[384,768]{1,0:T(8,128)(2,1)}, u32[]{:S(2)}) copy-start(bf16[384,768]{1,0:T(8,128)(2,1)} %w_ref.3) | copy-start | bytes 1769476
  5.5 49.8 %all-to-all-start = ((bf16[16,4,16,768]{3,2,1,0:T(8,128)(2,1)}), bf16[16,4,16,768]{3,2,1,0:T(8,128)(2,1)S(1)}, u32[]{:S(2)}, u32[]{:S(2)}) async-start(bf16[16,4,16,768]{3,2,1,0:T(8,128)(2,1)} %bitcast.12), calls=%async_computation | async-start | bytes 3145728 | tf_op jit(solution)/shard_map/all_to_all | solution.py:211
  15.2 34.8 %collective-permute-start = (bf16[3,192,768]{2,1,0:T(8,128)(2,1)}, bf16[3,192,768]{2,1,0:T(8,128)(2,1)S(1)}, u32[]{:S(2)}, u32[]{:S(2)}) collective-permute-start(bf16[3,192,768]{2,1,0:T(8,128)(2,1)} %dynamic-slice_bitcast_fusion), channel_id=1, source_target_pairs={{0,1},{1,0},{2,3},{3,2},{4,5},{5,4},{6,7},{7,6},{8,9},{9,8},{10,11... | collective-permute-start | bytes 2654216 | tf_op jit(solution)/shard_map/ppermute | solution.py:179
  18.4 30.0 %collective-permute-start.2 = (bf16[384,384]{1,0:T(8,128)(2,1)}, bf16[384,384]{1,0:T(8,128)(2,1)S(1)}, u32[]{:S(2)}, u32[]{:S(2)}) collective-permute-start(bf16[384,384]{1,0:T(8,128)(2,1)} %constant_dynamic-slice_fusion.1), channel_id=1, source_target_pairs={{0,1},{1,0},{2,3},{3,2},{4,5},{5,4},{6,7},{7,6},{8,9},{9,8},{10,11... | collective-permute-start | bytes 884744 | tf_op jit(solution)/shard_map/ppermute | solution.py:179
  19.7 30.3 %collective-permute-start.5 = (bf16[192,768]{1,0:T(8,128)(2,1)}, bf16[192,768]{1,0:T(8,128)(2,1)S(1)}, u32[]{:S(2)}, u32[]{:S(2)}) collective-permute-start(bf16[192,768]{1,0:T(8,128)(2,1)} %constant_dynamic-slice_fusion), channel_id=1, source_target_pairs={{0,1},{1,0},{2,3},{3,2},{4,5},{5,4},{6,7},{7,6},{8,9},{9,8},{10,11... | collective-permute-start | bytes 884744 | tf_op jit(solution)/shard_map/ppermute | solution.py:179
  55.3 6.3 %copy-start.13 = (bf16[384,384]{1,0:T(8,128)(2,1)S(1)}, bf16[384,384]{1,0:T(8,128)(2,1)}, u32[]{:S(2)}) copy-start(bf16[384,384]{1,0:T(8,128)(2,1)} %copy-done.12) | copy-start | bytes 884740
  55.3 6.5 %copy-start.14 = (s32[256]{0:T(256)S(1)}, s32[256]{0:T(256)}, u32[]{:S(2)}) copy-start(s32[256]{0:T(256)} %param.13) | copy-start | bytes 3076
  55.3 9.1 %copy-start.6 = (bf16[16,4,16,768]{3,2,1,0:T(8,128)(2,1)}, bf16[16,4,16,768]{3,2,1,0:T(8,128)(2,1)S(1)}, u32[]{:S(2)}) copy-start(bf16[16,4,16,768]{3,2,1,0:T(8,128)(2,1)S(1)} %all-to-all-done.x_ref) | copy-start | bytes 4718596
  55.3 37.7 %all-to-all-start.2 = ((bf16[16,4,16,768]{3,2,1,0:T(8,128)(2,1)}), bf16[16,4,16,768]{3,2,1,0:T(8,128)(2,1)S(1)}, u32[]{:S(2)}, u32[]{:S(2)}) async-start(bf16[16,4,16,768]{3,2,1,0:T(8,128)(2,1)} %bitcast.11), calls=%async_computation.2 | async-start | bytes 3145728 | tf_op jit(solution)/shard_map/all_to_all | solution.py:211
  61.2 3.3 %collective-permute-start.1 = (bf16[3,192,768]{2,1,0:T(8,128)(2,1)}, bf16[3,192,768]{2,1,0:T(8,128)(2,1)}, u32[]{:S(2)}, u32[]{:S(2)}) collective-permute-start(bf16[3,192,768]{2,1,0:T(8,128)(2,1)} %copy-done.9), channel_id=1, source_target_pairs={{0,2},{2,0},{4,6},{6,4},{8,10},{10,8},{12,14},{14,12},{16,18},{18,... | collective-permute-start | bytes 2654216 | tf_op jit(solution)/shard_map/ppermute | solution.py:180
  61.6 2.8 %collective-permute-start.3 = (bf16[384,384]{1,0:T(8,128)(2,1)S(1)}, bf16[384,384]{1,0:T(8,128)(2,1)}, u32[]{:S(2)}, u32[]{:S(2)}) collective-permute-start(bf16[384,384]{1,0:T(8,128)(2,1)S(1)} %copy-done.13), channel_id=1, source_target_pairs={{0,2},{2,0},{4,6},{6,4},{8,10},{10,8},{12,14},{14,12},{16,18},{18,... | collective-permute-start | bytes 884744 | tf_op jit(solution)/shard_map/ppermute | solution.py:180
  93.0 9.1 %copy-start.7 = (bf16[16,4,16,768]{3,2,1,0:T(8,128)(2,1)}, bf16[16,4,16,768]{3,2,1,0:T(8,128)(2,1)S(1)}, u32[]{:S(2)}) copy-start(bf16[16,4,16,768]{3,2,1,0:T(8,128)(2,1)S(1)} %all-to-all-done.2.x_ref) | copy-start | bytes 4718596
  93.0 41.0 %all-to-all-start.1 = ((bf16[16,4,16,768]{3,2,1,0:T(8,128)(2,1)}), bf16[16,4,16,768]{3,2,1,0:T(8,128)(2,1)S(1)}, u32[]{:S(2)}, u32[]{:S(2)}) async-start(bf16[16,4,16,768]{3,2,1,0:T(8,128)(2,1)} %group_path.2._), calls=%async_computation.1 | async-start | bytes 3145728 | tf_op jit(solution)/shard_map/all_to_all | solution.py:289
  117.4 27.3 %copy-start.5 = (bf16[192,768]{1,0:T(8,128)(2,1)S(1)}, bf16[192,768]{1,0:T(8,128)(2,1)}, u32[]{:S(2)}) copy-start(bf16[192,768]{1,0:T(8,128)(2,1)} %copy-done.4) | copy-start | bytes 884740
  134.0 46.2 %copy-start = (bf16[16,4,16,768]{3,2,1,0:T(8,128)(2,1)}, bf16[16,4,16,768]{3,2,1,0:T(8,128)(2,1)S(1)}, u32[]{:S(2)}) copy-start(bf16[16,4,16,768]{3,2,1,0:T(8,128)(2,1)S(1)} %all-to-all-done.1) | copy-start | bytes 4718596
  134.0 53.6 %all-to-all-start.3 = ((bf16[16,4,16,768]{3,2,1,0:T(8,128)(2,1)}), bf16[16,4,16,768]{3,2,1,0:T(8,128)(2,1)S(1)}, u32[]{:S(2)}, u32[]{:S(2)}) async-start(bf16[16,4,16,768]{3,2,1,0:T(8,128)(2,1)} %group_path.3), calls=%async_computation.3 | async-start | bytes 3145728 | tf_op jit(solution)/shard_map/all_to_all | solution.py:289
  143.1 37.1 %collective-permute-start.4 = (bf16[16,128,384]{2,1,0:T(8,128)(2,1)}, bf16[16,128,384]{2,1,0:T(8,128)(2,1)}, u32[]{:S(2)}, u32[]{:S(2)}) collective-permute-start(bf16[16,128,384]{2,1,0:T(8,128)(2,1)} %get-tuple-element.12), channel_id=1, source_target_pairs={{0,1},{1,0},{2,3},{3,2},{4,5},{5,4},{6,7},{7,6},{8,9},{9,8},{10,11... | collective-permute-start | bytes 4718600 | tf_op jit(solution)/shard_map/ppermute | solution.py:248
  144.7 1.6 collective-permute-start.6
  146.3 33.9 %copy-start.8 = (bf16[192,768]{1,0:T(8,128)(2,1)}, bf16[192,768]{1,0:T(8,128)(2,1)S(1)}, u32[]{:S(2)}) copy-start(bf16[192,768]{1,0:T(8,128)(2,1)S(1)} %collective-permute-done.6.wb_ref) | copy-start | bytes 884740
  186.1 20.6 %collective-permute-start.7 = (bf16[16,64,384]{2,1,0:T(8,128)(2,1)}, bf16[16,64,384]{2,1,0:T(8,128)(2,1)S(1)}, u32[]{:S(2)}, u32[]{:S(2)}) collective-permute-start(bf16[16,64,384]{2,1,0:T(8,128)(2,1)} %get-tuple-element.14), channel_id=1, source_target_pairs={{0,1},{1,0},{2,3},{3,2},{4,5},{5,4},{6,7},{7,6},{8,9},{9,8},{10,11... | collective-permute-start | bytes 2359304 | tf_op jit(solution)/shard_map/ppermute | solution.py:317
  188.8 7.0 %copy-start.10 = (bf16[16,64,384]{2,1,0:T(8,128)(2,1)S(1)}, bf16[16,64,384]{2,1,0:T(8,128)(2,1)}, u32[]{:S(2)}) copy-start(bf16[16,64,384]{2,1,0:T(8,128)(2,1)} %get-tuple-element.13) | copy-start | bytes 2359300
  194.8 27.4 %collective-permute-start.8 = (bf16[16,64,384]{2,1,0:T(8,128)(2,1)}, bf16[16,64,384]{2,1,0:T(8,128)(2,1)S(1)}, u32[]{:S(2)}, u32[]{:S(2)}) collective-permute-start(bf16[16,64,384]{2,1,0:T(8,128)(2,1)} %get-tuple-element.16), channel_id=1, source_target_pairs={{0,1},{1,0},{2,3},{3,2},{4,5},{5,4},{6,7},{7,6},{8,9},{9,8},{10,11... | collective-permute-start | bytes 2359304 | tf_op jit(solution)/shard_map/ppermute | solution.py:317
  195.3 11.6 %copy-start.11 = (bf16[16,64,384]{2,1,0:T(8,128)(2,1)S(1)}, bf16[16,64,384]{2,1,0:T(8,128)(2,1)}, u32[]{:S(2)}) copy-start(bf16[16,64,384]{2,1,0:T(8,128)(2,1)} %get-tuple-element.15) | copy-start | bytes 2359300
  207.1 15.1 %copy-start.3 = (bf16[16,256,384]{2,1,0:T(8,128)(2,1)}, bf16[16,256,384]{2,1,0:T(8,128)(2,1)S(1)}, u32[]{:S(2)}) copy-start(bf16[16,256,384]{2,1,0:T(8,128)(2,1)S(1)} %constant_dynamic-update-slice_fusion.1) | copy-start | bytes 9437188
  (4 other events, 4.5 us)

commit v3 on v2

--- a/solution.py
+++ b/solution.py
@@ -8,7 +8,8 @@
 from jax.sharding import PartitionSpec as P
 
 
-CHUNKS = 2
+SHARES = (3, 3, 2)
+FIRST_SERIES = (3, 8)
 VMEM_BYTES = 60 * 1024 * 1024
 
 
@@ -58,11 +59,12 @@
 
 def prep_kernel(_, x_ref, gain_ref, *rest):
     out_ref = rest[-1]
-    normed = rms_norm(x_ref[...], gain_ref[...].reshape(1, 1, -1)).astype(jnp.float32)
+    normed = rms_norm(x_ref[...], gain_ref[...]).astype(jnp.float32)
     out_ref[...] = jnp.swapaxes(normed, 0, 1).astype(jnp.bfloat16)
 
 
-def time_kernel(x_ref, gain_ref, w_ref, _, own_ref, give_ref, made_ref, *, head_size):
+def time_kernel(x_ref, gain_ref, w_ref, *rest, head_size):
+    own_ref, give_ref, made_ref = rest[-3:]
     is_low = lax.axis_index("mp") == 0
     width = own_ref.shape[-1]
     half = own_ref.shape[1]
@@ -127,7 +129,7 @@
             out_ref[:, 0, :, to : to + pair] = got.reshape(sources, ser_local, pair)
 
 
-def join_kernel(group_ref, own_ref, other_ref, w_ref, wa_ref, wb_ref, keep_ref, send_ref, full_ref):
+def join_kernel(group_ref, own_a, own_b, other_a, other_b, w_ref, wa_ref, wb_ref, keep_ref, send_ref, full_ref):
     me = lax.axis_index("mp")
     core = lax.axis_index("series") % 2
     block, ser_local, width = group_ref.shape
@@ -142,8 +144,8 @@
             full_ref[pl.ds(to, quarter)] = part[...]
 
     group = jnp.swapaxes(group_ref[...].astype(jnp.float32), 0, 1).reshape(ser_local * block, width)
-    own = own_ref[...].reshape(ser_local * block, half).astype(jnp.float32)
-    other = other_ref[...].reshape(ser_local * block, half).astype(jnp.float32)
+    own = jnp.concatenate([own_a[...], own_b[...]], axis=0).reshape(ser_local * block, half).astype(jnp.float32)
+    other = jnp.concatenate([other_a[...], other_b[...]], axis=0).reshape(ser_local * block, half).astype(jnp.float32)
     is_low = me == 0
     low = jnp.where(is_low, own, other)
     high = jnp.where(is_low, other, own)
@@ -179,14 +181,14 @@
         first = lax.ppermute(part, "mp", swap)
         return first, lax.ppermute(first, "series", sibling)
 
-    step = each // CHUNKS
+    steps = [each * share // sum(SHARES) for share in SHARES]
+    starts = [ns * sum(steps[:c]) for c in range(len(steps))]
     block = 16
-    gain = norm_gain.reshape(1, depth)
     me_ref = me.astype(jnp.int32).reshape(1)
     sent, received = [], []
-    chunk = ns * step
 
     def send_chunk(c, after):
+        step, chunk = steps[c], ns * steps[c]
         piece = pl.pallas_call(
             prep_kernel,
             grid_spec=pltpu.PrefetchScalarGridSpec(
@@ -195,9 +197,9 @@
                 in_specs=[
                     pl.BlockSpec(
                         (ser_local, block, depth),
-                        lambda i, m, c=c: (0, (m[0] * half + c * chunk) // block + i, 0),
+                        lambda i, m, c=c: (0, (m[0] * half + starts[c]) // block + i, 0),
                     ),
-                    whole(1, depth),
+                    whole(depth),
                     *[unread] * len(after),
                 ],
                 out_specs=pl.BlockSpec((block, ser_local, depth), lambda i, m: (i, 0, 0)),
@@ -205,7 +207,7 @@
             out_shape=jax.ShapeDtypeStruct((chunk, ser_local, depth), jnp.bfloat16),
             compiler_params=params(),
             name="prep_path",
-        )(me_ref, series_in, gain, *after)
+        )(me_ref, series_in, norm_gain, *after)
         sent.append(piece)
         received.append(
             lax.all_to_all(
@@ -222,35 +224,44 @@
     gate_a, gate_b = from_partner(w_gate)
     out_a, out_b = from_partner(w_out)
 
-    time_own, time_give = pl.pallas_call(
-        partial(time_kernel, head_size=head_size),
-        grid=(ser_local,),
-        in_specs=[
-            pl.BlockSpec((1, patches, depth), lambda i: (i, 0, 0)),
-            whole(1, depth),
-            whole(heads_local, 3 * head_size, depth),
-            unread,
-        ],
-        out_specs=[pl.BlockSpec((1, half, width), lambda i: (i, 0, 0))] * 2,
-        out_shape=[jax.ShapeDtypeStruct((ser_local, half, width), jnp.bfloat16)] * 2,
-        scratch_shapes=[pltpu.VMEM((1, 3 * width, depth), jnp.bfloat16)],
-        compiler_params=params(),
-        name="time_path",
-        cost_estimate=pl.CostEstimate(
-            flops=2 * ser_local * patches * (depth * 3 * width + 4 * patches * width),
-            bytes_accessed=ser_local * patches * (depth + width) * 2,
-            transcendentals=ser_local * heads_local * patches * patches,
-        ),
-    )(series_in, gain, turned(w_time), sent[0])
-    for c in range(1, CHUNKS):
-        send_chunk(c, (time_own, group_a, gate_a, out_a) if c == 1 else (sent[-1],))
-
-    time_other = lax.ppermute(time_give, "mp", swap)
-
+    first_count = ser_local * FIRST_SERIES[0] // FIRST_SERIES[1]
+    time_own, time_other = [], []
+
+    def time_call(at, count, after):
+        call = pl.pallas_call(
+            partial(time_kernel, head_size=head_size),
+            grid=(count,),
+            in_specs=[
+                pl.BlockSpec((1, patches, depth), lambda i: (at + i, 0, 0)),
+                whole(depth),
+                whole(heads_local, 3 * head_size, depth),
+                *[unread] * len(after),
+            ],
+            out_specs=[pl.BlockSpec((1, half, width), lambda i: (i, 0, 0))] * 2,
+            out_shape=[jax.ShapeDtypeStruct((count, half, width), jnp.bfloat16)] * 2,
+            scratch_shapes=[pltpu.VMEM((1, 3 * width, depth), jnp.bfloat16)],
+            compiler_params=params(),
+            name="time_path",
+            cost_estimate=pl.CostEstimate(
+                flops=2 * count * patches * (depth * 3 * width + 4 * patches * width),
+                bytes_accessed=count * patches * (depth + width) * 2,
+                transcendentals=count * heads_local * patches * patches,
+            ),
+        )
+        own, give = call(series_in, norm_gain, turned(w_time), *after)
+        time_other.append(lax.ppermute(give, "mp", swap))
+        time_own.append(own)
+
+    send_chunk(1, (sent[0],))
+    time_call(0, first_count, (sent[1],))
+    send_chunk(2, (time_own[0],))
+    time_call(first_count, ser_local - first_count, (sent[2], group_a, gate_a, out_a))
+
+    counts = [first_count, ser_local - first_count]
     out = jnp.zeros((ser_local, patches, width), jnp.bfloat16)
-    last = time_own
+    last = time_own[1]
     backs = []
-    for c in range(CHUNKS):
+    for c, step in enumerate(steps):
         call = pl.pallas_call(
             partial(group_kernel, head_size=head_size),
             grid=(step,),
@@ -285,20 +296,18 @@
         group_of.reshape(n_series, 1), group_of.reshape(1, n_series), last,
         )
         last = group_out
-        backs.append(
-            lax.all_to_all(group_out, "series", split_axis=0, concat_axis=0, tiled=True)
-        )
-
-    for c in range(CHUNKS):
+        backs.append(lax.all_to_all(group_out, "series", split_axis=0, concat_axis=0, tiled=True))
+
+    for c, step in enumerate(steps):
+        chunk = ns * step
         back = backs[c].reshape(chunk, ser_local, total)
-        at_chunk = lambda i, c=c: (0, c * chunk // block + i, 0)
-        keep, give = pl.pallas_call(
+        at_chunk = lambda i, c=c: (0, starts[c] // block + i, 0)
+        call = pl.pallas_call(
             join_kernel,
             grid=(chunk // block,),
             in_specs=[
                 pl.BlockSpec((block, ser_local, total), lambda i: (i, 0, 0)),
-                pl.BlockSpec((ser_local, block, width), at_chunk),
-                pl.BlockSpec((ser_local, block, width), at_chunk),
+                *[pl.BlockSpec((n, block, width), at_chunk) for n in counts * 2],
                 whole(*w_out.shape),
                 whole(*out_a.shape),
                 whole(*out_b.shape),
@@ -313,10 +322,11 @@
                 bytes_accessed=4 * chunk * ser_local * total * 2,
                 transcendentals=0,
             ),
-        )(back, time_own, time_other, w_out, out_a, out_b)
+        )
+        keep, give = call(back, *time_own, *time_other, w_out, out_a, out_b)
         taken = lax.ppermute(give, "mp", swap)
-        out = lax.dynamic_update_slice_in_dim(out, keep, me * half + c * chunk, 1)
-        out = lax.dynamic_update_slice_in_dim(out, taken, (nm - 1 - me) * half + c * chunk, 1)
+        out = lax.dynamic_update_slice_in_dim(out, keep, me * half + starts[c], 1)
+        out = lax.dynamic_update_slice_in_dim(out, taken, (nm - 1 - me) * half + starts[c], 1)
     return out
 
 
@@ -391,8 +401,8 @@
     ser_local, patches, _ = series_in.shape
     ns, nm = lax.axis_size("series"), lax.axis_size("mp")
     pairs = w_time.shape[1] % 2 == 0 and w_time.shape[2] % 48 == 0 and (2 * w_time.shape[2] // 3) % 128 == 0
-    tiled = ser_local % 16 == 0 and patches % (ns * nm * CHUNKS) == 0 and patches // nm % (16 * CHUNKS) == 0
-    tiled = tiled and ns % 2 == 0 and w_time.shape[0] % 32 == 0
+    tiled = ser_local % 16 == 0 and patches % (ns * nm * sum(SHARES)) == 0
+    tiled = tiled and ns % 16 == 0 and w_time.shape[0] % 32 == 0
     if nm == 2 and pairs and tiled:
         return split_patches(series_in, norm_gain, w_time, *rest)
     return split_heads(series_in, norm_gain, w_time, *rest)

time: 224 us -> 287 us (1.28)
  blocking collectives: 0 us -> 35.6 us
  waiting for transfers between devices: 94.7 us -> 112 us
  Pallas kernels: 78.2 us -> 87.5 us
    all_to_all x0 -> x1, blocking collectives: none -> 35.6 us  [split_patches(): lax.all_to_all(group_out, 'series', split_axis=0, concat_axis=0, tiled=True)]
    ppermute x3, waiting for transfers between devices: 1.59 us -> 18.2 us  [from_partner(): first = lax.ppermute(part, 'mp', swap)]
    all_to_all x2 -> x3, waiting for transfers between devices: 13.3 us -> 21.4 us  [send_chunk(): lax.all_to_all(piece.reshape(ns, step, ser_local, depth), 'series', split...]
    all_to_all x2 -> x3, starting transfers between devices: 13.4 us -> 20.8 us  [send_chunk(): lax.all_to_all(piece.reshape(ns, step, ser_local, depth), 'series', split...]
    all_to_all x2, starting transfers between devices: 18.2 us -> 11.1 us  [split_patches(): lax.all_to_all(group_out, 'series', split_axis=0, concat_axis=0, tiled=True)]
    pallas_call x3 -> x5, Pallas kernels: 39.1 us -> 43.7 us  [the longest x2 29.7 us: time_call(): own, give = call(series_in, norm_gain, turned(w_time), *after)]
    ppermute x2 -> x3, waiting for transfers between devices: 25.9 us -> 21.5 us  [split_patches(): taken = lax.ppermute(give, 'mp', swap)]
    pallas_call x2 -> x3, Pallas kernels: 30.5 us -> 34 us  [split_patches(): call(received[c], group_own, group_a, group_b, w_gate, gate_a, gate_b, gr...]
  transfers between devices with their start and end apart: 13 -> 16, of which waited for: 8 -> 8; matrix products, arithmetic and copies ran while one was open for 3% -> 2% of each run, Pallas kernels for 33% -> 29%
where the time goes in v3:
time: 287 us; the launch traced here: 286 us
  waiting for transfers between devices  112 us (39%)
  Pallas kernels  87.5 us (30%)
  starting transfers between devices  41.7 us (15%)
  blocking collectives  35.6 us (12%)
  local copies, waits for them, and re-layouts  9.1 us (3%)
    all_to_all x1, blocking collectives, split_patches(): lax.all_to_all(group_out, 'series', split_axis=0, concat_axis=0, tiled=True)  35.6 us
    pallas_call x3, Pallas kernels, split_patches(): call(received[c], group_own, group_a, group_b, w_gate, gate_a, gate_b, gr...  34 us
    ppermute x2, waiting for transfers between devices, time_call(): time_other.append(lax.ppermute(give, 'mp', swap))  33 us
    pallas_call x2, Pallas kernels, time_call(): own, give = call(series_in, norm_gain, turned(w_time), *after)  29.7 us
    ppermute x3, waiting for transfers between devices, split_patches(): taken = lax.ppermute(give, 'mp', swap)  21.5 us
    all_to_all x3, waiting for transfers between devices, send_chunk(): lax.all_to_all(piece.reshape(ns, step, ser_local, depth), 'series', split...  21.4 us
    all_to_all x3, starting transfers between devices, send_chunk(): lax.all_to_all(piece.reshape(ns, step, ser_local, depth), 'series', split...  20.8 us
    ppermute x3, waiting for transfers between devices, from_partner(): first = lax.ppermute(part, 'mp', swap)  18.2 us
  transfers between devices with their start and end apart: 16, of which 8 were waited for; matrix products, arithmetic and copies ran while one was open for 2% of the time, Pallas kernels for 29%

profile of v3, /device:TPU:0, one launch (start us, length us, event | category | flops | bytes accessed | tf_op | source)
XLA Modules:
  0.0 285.8 jit_solution(1802784832146135256)
XLA Ops:
  0.0 3.6 %prep_path.3.rest_0_ = bf16[48,16,768]{2,1,0:T(8,128)(2,1)} custom-call(s32[1]{0:T(128)} %bitcast._, bf16[16,256,768]{2,1,0:T(8,128)(2,1)} %x_ref.9, f32[768]{0:T(1024)} %gain_ref.9), custom_call_target="tpu_custom_call" | custom-call | tf_op jit(solution)/shard_map/prep_path/pallas_call | solution.py:192
  3.6 7.4 %all-to-all-start = ((bf16[16,3,16,768]{3,2,1,0:T(8,128)(2,1)}), bf16[16,3,16,768]{3,2,1,0:T(8,128)(2,1)S(1)}, u32[]{:S(2)}, u32[]{:S(2)}) async-start(bf16[16,3,16,768]{3,2,1,0:T(8,128)(2,1)} %bitcast.13), calls=%async_computation | async-start | bytes 2359296 | tf_op jit(solution)/shard_map/all_to_all | solution.py:213
  11.0 3.7 %prep_path.4.rest_0_ = bf16[48,16,768]{2,1,0:T(8,128)(2,1)} custom-call(s32[1]{0:T(128)} %bitcast._, bf16[16,256,768]{2,1,0:T(8,128)(2,1)} %x_ref.9, f32[768]{0:T(1024)} %gain_ref.9, bf16[48,16,768]{2,1,0:T(8,128)(2,1)} %prep_path.3.rest_0_), custom_call_target="tpu_custom_call" | custom-call | tf_op jit(solution)/shard_map/prep_path/pallas_call | solution.py:192
  14.7 21.4 %all-to-all-done.x_ref = bf16[16,3,16,768]{3,2,1,0:T(8,128)(2,1)S(1)} async-done(((bf16[16,3,16,768]{3,2,1,0:T(8,128)(2,1)}), bf16[16,3,16,768]{3,2,1,0:T(8,128)(2,1)S(1)}, u32[]{:S(2)}, u32[]{:S(2)}) %all-to-all-start) | async-done | bytes 1179680 | tf_op jit(solution)/shard_map/all_to_all | solution.py:213
  36.1 7.4 %all-to-all-start.2 = ((bf16[16,3,16,768]{3,2,1,0:T(8,128)(2,1)}), bf16[16,3,16,768]{3,2,1,0:T(8,128)(2,1)S(1)}, u32[]{:S(2)}, u32[]{:S(2)}) async-start(bf16[16,3,16,768]{3,2,1,0:T(8,128)(2,1)} %bitcast.14), calls=%async_computation.2 | async-start | bytes 2359296 | tf_op jit(solution)/shard_map/all_to_all | solution.py:213
  50.4 18.2 %collective-permute-done.rest_1_.wa_ref = bf16[3,192,768]{2,1,0:T(8,128)(2,1)} collective-permute-done((bf16[3,192,768]{2,1,0:T(8,128)(2,1)}, bf16[3,192,768]{2,1,0:T(8,128)(2,1)}, u32[]{:S(2)}, u32[]{:S(2)}) %collective-permute-start) | collective-permute-done | bytes 884768 | tf_op jit(solution)/shard_map/ppermute | solution.py:181
  68.6 11.7 %time_path.2 = (bf16[6,128,384]{2,1,0:T(8,128)(2,1)}, bf16[6,128,384]{2,1,0:T(8,128)(2,1)}) custom-call(bf16[16,256,768]{2,1,0:T(8,128)(2,1)} %x_ref.9, f32[768]{0:T(1024)} %gain_ref.9, bf16[6,192,768]{2,1,0:T(8,128)(2,1)} %bitcast.26, bf16[48,16,768]{2,1,0:T(8,128)(2,1)} %prep_path.4.rest_0_), custom_call_target="tpu_custom_call" | custom-call | flops 3925868544 | bytes 3538944 | tf_op jit(solution)/shard_map/time_path/pallas_call | solution.py:251
  80.3 2.5 prep_path.5.rest_0_
  84.1 6.0 %all-to-all-start.4 = ((bf16[16,2,16,768]{3,2,1,0:T(8,128)(2,1)}), bf16[16,2,16,768]{3,2,1,0:T(8,128)(2,1)S(1)}, u32[]{:S(2)}, u32[]{:S(2)}) async-start(bf16[16,2,16,768]{3,2,1,0:T(8,128)(2,1)} %bitcast.18), calls=%async_computation.4 | async-start | bytes 1572864 | tf_op jit(solution)/shard_map/all_to_all | solution.py:213
  90.8 18.0 %time_path.3 = (bf16[10,128,384]{2,1,0:T(8,128)(2,1)}, bf16[10,128,384]{2,1,0:T(8,128)(2,1)}) custom-call(bf16[16,256,768]{2,1,0:T(8,128)(2,1)} %x_ref.9, f32[768]{0:T(1024)} %gain_ref.9, bf16[6,192,768]{2,1,0:T(8,128)(2,1)} %bitcast.27, bf16[32,16,768]{2,1,0:T(8,128)(2,1)} %prep_path.5.rest_0_, bf16[3,192,768]{2,1,0:T(8,128)(2,1)} %collective-permute-done.rest_1_.wa_ref, ...), custom_call_target="tpu_custom_call" | custom-call | flops 6543114240 | bytes 5898240 | tf_op jit(solution)/shard_map/time_path/pallas_call | solution.py:251
  109.5 12.3 %group_path.3._ = bf16[16,3,16,768]{3,2,1,0:T(8,128)(2,1)} custom-call(bf16[16,3,16,768]{3,2,1,0:T(8,128)(2,1)} %copy-done.8, bf16[6,192,768]{2,1,0:T(8,128)(2,1)} %bitcast.19, bf16[3,192,768]{2,1,0:T(8,128)(2,1)} %collective-permute-done.rest_1_.wa_ref, bf16[3,192,768]{2,1,0:T(8,128)(2,1)} %collective-permute-done.1.wb_ref, bf16[768,384]{1,0:T(8,128)(2,1)} %g_ref.5, ...), custom_call_target="tpu_custom_call" | custom-call | flops 4831838208 | bytes 2359296 | tf_op jit(solution)/shard_map/group_path/pallas_call | solution.py:294
  121.8 12.3 %group_path.4._ = bf16[16,3,16,768]{3,2,1,0:T(8,128)(2,1)} custom-call(bf16[16,3,16,768]{3,2,1,0:T(8,128)(2,1)} %copy-done.9, bf16[6,192,768]{2,1,0:T(8,128)(2,1)} %bitcast.20, bf16[3,192,768]{2,1,0:T(8,128)(2,1)} %collective-permute-done.rest_1_.wa_ref, bf16[3,192,768]{2,1,0:T(8,128)(2,1)} %collective-permute-done.1.wb_ref, bf16[768,384]{1,0:T(8,128)(2,1)} %g_ref.5, ...), custom_call_target="tpu_custom_call" | custom-call | flops 4831838208 | bytes 2359296 | tf_op jit(solution)/shard_map/group_path/pallas_call | solution.py:294
  134.1 35.6 %all_to_all.30 = bf16[16,3,16,768]{3,2,1,0:T(8,128)(2,1)} all-to-all(bf16[16,3,16,768]{3,2,1,0:T(8,128)(2,1)} %group_path.4._), channel_id=1, replica_groups=mesh['series'=16,'mp'=2] {'series'}, dimensions={0} | all-to-all | bytes 2359296 | tf_op jit(solution)/shard_map/all_to_all | solution.py:299
  169.7 3.7 %all-to-all-start.1 = ((bf16[16,3,16,768]{3,2,1,0:T(8,128)(2,1)}), bf16[16,3,16,768]{3,2,1,0:T(8,128)(2,1)S(1)}, u32[]{:S(2)}, u32[]{:S(2)}) async-start(bf16[16,3,16,768]{3,2,1,0:T(8,128)(2,1)} %group_path.3._), calls=%async_computation.1 | async-start | bytes 2359296 | tf_op jit(solution)/shard_map/all_to_all | solution.py:299
  173.4 9.4 %group_path.5 = bf16[16,2,16,768]{3,2,1,0:T(8,128)(2,1)} custom-call(bf16[16,2,16,768]{3,2,1,0:T(8,128)(2,1)} %copy-done.10, bf16[6,192,768]{2,1,0:T(8,128)(2,1)} %bitcast.21, bf16[3,192,768]{2,1,0:T(8,128)(2,1)} %collective-permute-done.rest_1_.wa_ref, bf16[3,192,768]{2,1,0:T(8,128)(2,1)} %collective-permute-done.1.wb_ref, bf16[768,384]{1,0:T(8,128)(2,1)} %g_ref.5, ...), custom_call_target="tpu_custom_call" | custom-call | flops 3221225472 | bytes 1572864 | tf_op jit(solution)/shard_map/group_path/pallas_call | solution.py:294
  182.8 15.6 %all-to-all-done.1 = bf16[16,3,16,768]{3,2,1,0:T(8,128)(2,1)S(1)} async-done(((bf16[16,3,16,768]{3,2,1,0:T(8,128)(2,1)}), bf16[16,3,16,768]{3,2,1,0:T(8,128)(2,1)S(1)}, u32[]{:S(2)}, u32[]{:S(2)}) %all-to-all-start.1) | async-done | bytes 1179680 | tf_op jit(solution)/shard_map/all_to_all | solution.py:299
  198.4 7.4 %all-to-all-start.5 = ((bf16[16,2,16,768]{3,2,1,0:T(8,128)(2,1)}), bf16[16,2,16,768]{3,2,1,0:T(8,128)(2,1)S(1)}, u32[]{:S(2)}, u32[]{:S(2)}) async-start(bf16[16,2,16,768]{3,2,1,0:T(8,128)(2,1)} %group_path.5), calls=%async_computation.5 | async-start | bytes 1572864 | tf_op jit(solution)/shard_map/all_to_all | solution.py:299
  209.7 33.0 %collective-permute-done.5.other_a = bf16[6,128,384]{2,1,0:T(8,128)(2,1)S(1)} collective-permute-done((bf16[6,128,384]{2,1,0:T(8,128)(2,1)}, bf16[6,128,384]{2,1,0:T(8,128)(2,1)S(1)}, u32[]{:S(2)}, u32[]{:S(2)}) %collective-permute-start.5) | collective-permute-done | bytes 589856 | tf_op jit(solution)/shard_map/ppermute | solution.py:252
  243.9 5.1 %join_path.3 = (bf16[16,48,384]{2,1,0:T(8,128)(2,1)}, bf16[16,48,384]{2,1,0:T(8,128)(2,1)}) custom-call(bf16[48,16,768]{2,1,0:T(8,128)(2,1)} %bitcast.16, bf16[6,128,384]{2,1,0:T(8,128)(2,1)} %get-tuple-element.15.rest_0_.own_a, bf16[10,128,384]{2,1,0:T(8,128)(2,1)} %get-tuple-element.16._.own_b, bf16[6,128,384]{2,1,0:T(8,128)(2,1)} %copy-done.2, ...), custom_call_target="tpu_custom_call" | custom-call | flops 905969664 | bytes 4718592 | tf_op jit(solution)/shard_map/join_path/pallas_call | solution.py:326
  250.5 5.1 %join_path.4 = (bf16[16,48,384]{2,1,0:T(8,128)(2,1)}, bf16[16,48,384]{2,1,0:T(8,128)(2,1)}) custom-call(bf16[48,16,768]{2,1,0:T(8,128)(2,1)} %bitcast.15, bf16[6,128,384]{2,1,0:T(8,128)(2,1)} %get-tuple-element.15.rest_0_.own_a, bf16[10,128,384]{2,1,0:T(8,128)(2,1)} %get-tuple-element.16._.own_b, bf16[6,128,384]{2,1,0:T(8,128)(2,1)} %copy-done.2, ...), custom_call_target="tpu_custom_call" | custom-call | flops 905969664 | bytes 4718592 | tf_op jit(solution)/shard_map/join_path/pallas_call | solution.py:326
  257.0 3.9 %join_path.5 = (bf16[16,32,384]{2,1,0:T(8,128)(2,1)}, bf16[16,32,384]{2,1,0:T(8,128)(2,1)}) custom-call(bf16[32,16,768]{2,1,0:T(8,128)(2,1)} %bitcast.17, bf16[6,128,384]{2,1,0:T(8,128)(2,1)} %get-tuple-element.15.rest_0_.own_a, bf16[10,128,384]{2,1,0:T(8,128)(2,1)} %get-tuple-element.16._.own_b, bf16[6,128,384]{2,1,0:T(8,128)(2,1)} %copy-done.2, ...), custom_call_target="tpu_custom_call" | custom-call | flops 603979776 | bytes 3145728 | tf_op jit(solution)/shard_map/join_path/pallas_call | solution.py:326
  263.0 2.4 collective-permute-done.8
  265.6 12.4 %collective-permute-done.9 = bf16[16,48,384]{2,1,0:T(8,128)(2,1)S(1)} collective-permute-done((bf16[16,48,384]{2,1,0:T(8,128)(2,1)}, bf16[16,48,384]{2,1,0:T(8,128)(2,1)S(1)}, u32[]{:S(2)}, u32[]{:S(2)}) %collective-permute-start.9) | collective-permute-done | bytes 589856 | tf_op jit(solution)/shard_map/ppermute | solution.py:327
  278.2 6.7 %collective-permute-done.10 = bf16[16,32,384]{2,1,0:T(8,128)(2,1)S(1)} collective-permute-done((bf16[16,32,384]{2,1,0:T(8,128)(2,1)}, bf16[16,32,384]{2,1,0:T(8,128)(2,1)S(1)}, u32[]{:S(2)}, u32[]{:S(2)}) %collective-permute-start.10) | collective-permute-done | bytes 393248 | tf_op jit(solution)/shard_map/ppermute | solution.py:327
  (63 shorter events, 20.7 us)
Async XLA Ops:
  3.6 32.5 %all-to-all-start = ((bf16[16,3,16,768]{3,2,1,0:T(8,128)(2,1)}), bf16[16,3,16,768]{3,2,1,0:T(8,128)(2,1)S(1)}, u32[]{:S(2)}, u32[]{:S(2)}) async-start(bf16[16,3,16,768]{3,2,1,0:T(8,128)(2,1)} %bitcast.13), calls=%async_computation | async-start | bytes 2359296 | tf_op jit(solution)/shard_map/all_to_all | solution.py:213
  14.7 34.1 %copy-start.1 = (bf16[384,768]{1,0:T(8,128)(2,1)S(1)}, bf16[384,768]{1,0:T(8,128)(2,1)}, u32[]{:S(2)}) copy-start(bf16[384,768]{1,0:T(8,128)(2,1)} %w_ref.5) | copy-start | bytes 1769476
  36.1 44.2 %copy-start.8 = (bf16[16,3,16,768]{3,2,1,0:T(8,128)(2,1)}, bf16[16,3,16,768]{3,2,1,0:T(8,128)(2,1)S(1)}, u32[]{:S(2)}) copy-start(bf16[16,3,16,768]{3,2,1,0:T(8,128)(2,1)S(1)} %all-to-all-done.x_ref) | copy-start | bytes 3538948
  36.1 48.0 %all-to-all-start.2 = ((bf16[16,3,16,768]{3,2,1,0:T(8,128)(2,1)}), bf16[16,3,16,768]{3,2,1,0:T(8,128)(2,1)S(1)}, u32[]{:S(2)}, u32[]{:S(2)}) async-start(bf16[16,3,16,768]{3,2,1,0:T(8,128)(2,1)} %bitcast.14), calls=%async_computation.2 | async-start | bytes 2359296 | tf_op jit(solution)/shard_map/all_to_all | solution.py:213
  45.7 22.8 %collective-permute-start = (bf16[3,192,768]{2,1,0:T(8,128)(2,1)}, bf16[3,192,768]{2,1,0:T(8,128)(2,1)}, u32[]{:S(2)}, u32[]{:S(2)}) collective-permute-start(bf16[3,192,768]{2,1,0:T(8,128)(2,1)} %dynamic-slice_bitcast_fusion), channel_id=1, source_target_pairs={{0,1},{1,0},{2,3},{3,2},{4,5},{5,4},{6,7},{7,6},{8,9},{9,8},{10,11... | collective-permute-start | bytes 2654216 | tf_op jit(solution)/shard_map/ppermute | solution.py:181
  48.2 35.4 %collective-permute-start.2 = (bf16[384,384]{1,0:T(8,128)(2,1)S(1)}, bf16[384,384]{1,0:T(8,128)(2,1)}, u32[]{:S(2)}, u32[]{:S(2)}) collective-permute-start(bf16[384,384]{1,0:T(8,128)(2,1)S(1)} %constant_dynamic-slice_fusion.1), channel_id=1, source_target_pairs={{0,1},{1,0},{2,3},{3,2},{4,5},{5,4},{6,7},{7,6},{8,9},{9,8},{10,11... | collective-permute-start | bytes 884744 | tf_op jit(solution)/shard_map/ppermute | solution.py:181
  48.8 41.3 %collective-permute-start.4 = (bf16[192,768]{1,0:T(8,128)(2,1)S(1)}, bf16[192,768]{1,0:T(8,128)(2,1)S(1)}, u32[]{:S(2)}, u32[]{:S(2)}) collective-permute-start(bf16[192,768]{1,0:T(8,128)(2,1)S(1)} %constant_dynamic-slice_fusion), channel_id=1, source_target_pairs={{0,1},{1,0},{2,3},{3,2},{4,5},{5,4},{6,7},{7,6},{8,9},{9,8},{10,11... | collective-permute-start | bytes 884744 | tf_op jit(solution)/shard_map/ppermute | solution.py:181
  68.5 40.2 %collective-permute-start.1 = (bf16[3,192,768]{2,1,0:T(8,128)(2,1)}, bf16[3,192,768]{2,1,0:T(8,128)(2,1)}, u32[]{:S(2)}, u32[]{:S(2)}) collective-permute-start(bf16[3,192,768]{2,1,0:T(8,128)(2,1)} %collective-permute-done.rest_1_.wa_ref), channel_id=1, source_target_pairs={{0,2},{2,0},{4,6},{6,4},{8,10},{10,8},{12,14},{14,12},{16,18},{18,... | collective-permute-start | bytes 2654216 | tf_op jit(solution)/shard_map/ppermute | solution.py:182
  83.6 25.2 %collective-permute-start.3 = (bf16[384,384]{1,0:T(8,128)(2,1)}, bf16[384,384]{1,0:T(8,128)(2,1)S(1)}, u32[]{:S(2)}, u32[]{:S(2)}) collective-permute-start(bf16[384,384]{1,0:T(8,128)(2,1)} %collective-permute-done.2.rest_2_.ga_ref), channel_id=1, source_target_pairs={{0,2},{2,0},{4,6},{6,4},{8,10},{10,8},{12,14},{14,12},{16,18},{18,... | collective-permute-start | bytes 884744 | tf_op jit(solution)/shard_map/ppermute | solution.py:182
  84.1 24.7 %copy-start.9 = (bf16[16,3,16,768]{3,2,1,0:T(8,128)(2,1)}, bf16[16,3,16,768]{3,2,1,0:T(8,128)(2,1)S(1)}, u32[]{:S(2)}) copy-start(bf16[16,3,16,768]{3,2,1,0:T(8,128)(2,1)S(1)} %all-to-all-done.2.x_ref) | copy-start | bytes 3538948
  84.1 50.0 %all-to-all-start.4 = ((bf16[16,2,16,768]{3,2,1,0:T(8,128)(2,1)}), bf16[16,2,16,768]{3,2,1,0:T(8,128)(2,1)S(1)}, u32[]{:S(2)}, u32[]{:S(2)}) async-start(bf16[16,2,16,768]{3,2,1,0:T(8,128)(2,1)} %bitcast.18), calls=%async_computation.4 | async-start | bytes 1572864 | tf_op jit(solution)/shard_map/all_to_all | solution.py:213
  134.1 35.6 %copy-start.10 = (bf16[16,2,16,768]{3,2,1,0:T(8,128)(2,1)}, bf16[16,2,16,768]{3,2,1,0:T(8,128)(2,1)S(1)}, u32[]{:S(2)}) copy-start(bf16[16,2,16,768]{3,2,1,0:T(8,128)(2,1)S(1)} %all-to-all-done.4.x_ref) | copy-start | bytes 2359300
  169.7 28.7 %all-to-all-start.1 = ((bf16[16,3,16,768]{3,2,1,0:T(8,128)(2,1)}), bf16[16,3,16,768]{3,2,1,0:T(8,128)(2,1)S(1)}, u32[]{:S(2)}, u32[]{:S(2)}) async-start(bf16[16,3,16,768]{3,2,1,0:T(8,128)(2,1)} %group_path.3._), calls=%async_computation.1 | async-start | bytes 2359296 | tf_op jit(solution)/shard_map/all_to_all | solution.py:299
  198.4 44.3 %copy-start.3 = (bf16[16,3,16,768]{3,2,1,0:T(8,128)(2,1)}, bf16[16,3,16,768]{3,2,1,0:T(8,128)(2,1)S(1)}, u32[]{:S(2)}) copy-start(bf16[16,3,16,768]{3,2,1,0:T(8,128)(2,1)S(1)} %all-to-all-done.1) | copy-start | bytes 3538948
  198.4 57.6 %all-to-all-start.5 = ((bf16[16,2,16,768]{3,2,1,0:T(8,128)(2,1)}), bf16[16,2,16,768]{3,2,1,0:T(8,128)(2,1)S(1)}, u32[]{:S(2)}, u32[]{:S(2)}) async-start(bf16[16,2,16,768]{3,2,1,0:T(8,128)(2,1)} %group_path.5), calls=%async_computation.5 | async-start | bytes 1572864 | tf_op jit(solution)/shard_map/all_to_all | solution.py:299
  205.8 36.9 %collective-permute-start.6 = (bf16[10,128,384]{2,1,0:T(8,128)(2,1)}, bf16[10,128,384]{2,1,0:T(8,128)(2,1)S(1)}, u32[]{:S(2)}, u32[]{:S(2)}) collective-permute-start(bf16[10,128,384]{2,1,0:T(8,128)(2,1)} %get-tuple-element.18), channel_id=1, source_target_pairs={{0,1},{1,0},{2,3},{3,2},{4,5},{5,4},{6,7},{7,6},{8,9},{9,8},{10,11... | collective-permute-start | bytes 2949128 | tf_op jit(solution)/shard_map/ppermute | solution.py:252
  207.4 35.4 %collective-permute-start.5 = (bf16[6,128,384]{2,1,0:T(8,128)(2,1)}, bf16[6,128,384]{2,1,0:T(8,128)(2,1)S(1)}, u32[]{:S(2)}, u32[]{:S(2)}) collective-permute-start(bf16[6,128,384]{2,1,0:T(8,128)(2,1)} %get-tuple-element.17), channel_id=1, source_target_pairs={{0,1},{1,0},{2,3},{3,2},{4,5},{5,4},{6,7},{7,6},{8,9},{9,8},{10,11... | collective-permute-start | bytes 1769480 | tf_op jit(solution)/shard_map/ppermute | solution.py:252
  207.9 1.8 collective-permute-start.7
  209.7 33.0 %copy-start.7 = (bf16[192,768]{1,0:T(8,128)(2,1)}, bf16[192,768]{1,0:T(8,128)(2,1)S(1)}, u32[]{:S(2)}) copy-start(bf16[192,768]{1,0:T(8,128)(2,1)S(1)} %collective-permute-done.7.wb_ref) | copy-start | bytes 884740
  249.0 16.4 %collective-permute-start.8 = (bf16[16,48,384]{2,1,0:T(8,128)(2,1)}, bf16[16,48,384]{2,1,0:T(8,128)(2,1)S(1)}, u32[]{:S(2)}, u32[]{:S(2)}) collective-permute-start(bf16[16,48,384]{2,1,0:T(8,128)(2,1)} %get-tuple-element.20), channel_id=1, source_target_pairs={{0,1},{1,0},{2,3},{3,2},{4,5},{5,4},{6,7},{7,6},{8,9},{9,8},{10,11... | collective-permute-start | bytes 1769480 | tf_op jit(solution)/shard_map/ppermute | solution.py:327
  255.5 22.5 %collective-permute-start.9 = (bf16[16,48,384]{2,1,0:T(8,128)(2,1)}, bf16[16,48,384]{2,1,0:T(8,128)(2,1)S(1)}, u32[]{:S(2)}, u32[]{:S(2)}) collective-permute-start(bf16[16,48,384]{2,1,0:T(8,128)(2,1)} %get-tuple-element.22), channel_id=1, source_target_pairs={{0,1},{1,0},{2,3},{3,2},{4,5},{5,4},{6,7},{7,6},{8,9},{9,8},{10,11... | collective-permute-start | bytes 1769480 | tf_op jit(solution)/shard_map/ppermute | solution.py:327
  260.8 24.1 %collective-permute-start.10 = (bf16[16,32,384]{2,1,0:T(8,128)(2,1)}, bf16[16,32,384]{2,1,0:T(8,128)(2,1)S(1)}, u32[]{:S(2)}, u32[]{:S(2)}) collective-permute-start(bf16[16,32,384]{2,1,0:T(8,128)(2,1)} %get-tuple-element.24), channel_id=1, source_target_pairs={{0,1},{1,0},{2,3},{3,2},{4,5},{5,4},{6,7},{7,6},{8,9},{9,8},{10,11... | collective-permute-start | bytes 1179656 | tf_op jit(solution)/shard_map/ppermute | solution.py:327
  262.8 15.3 %copy-start.13 = (bf16[16,32,384]{2,1,0:T(8,128)(2,1)S(1)}, bf16[16,32,384]{2,1,0:T(8,128)(2,1)}, u32[]{:S(2)}) copy-start(bf16[16,32,384]{2,1,0:T(8,128)(2,1)} %get-tuple-element.23) | copy-start | bytes 1179652
  278.2 6.7 %copy-start.5 = (bf16[16,256,384]{2,1,0:T(8,128)(2,1)}, bf16[16,256,384]{2,1,0:T(8,128)(2,1)S(1)}, u32[]{:S(2)}) copy-start(bf16[16,256,384]{2,1,0:T(8,128)(2,1)S(1)} %constant_dynamic-update-slice_fusion.1) | copy-start | bytes 9437188
  (8 other events, 17.3 us)

commit v4 on v3

--- a/solution.py
+++ b/solution.py
@@ -8,8 +8,7 @@
 from jax.sharding import PartitionSpec as P
 
 
-SHARES = (3, 3, 2)
-FIRST_SERIES = (3, 8)
+SHARES = (5, 3)
 VMEM_BYTES = 60 * 1024 * 1024
 
 
@@ -129,7 +128,9 @@
             out_ref[:, 0, :, to : to + pair] = got.reshape(sources, ser_local, pair)
 
 
-def join_kernel(group_ref, own_a, own_b, other_a, other_b, w_ref, wa_ref, wb_ref, keep_ref, send_ref, full_ref):
+def join_kernel(
+    group_ref, own_ref, other_ref, w_ref, wa_ref, wb_ref, keep_ref, send_ref, full_ref
+):
     me = lax.axis_index("mp")
     core = lax.axis_index("series") % 2
     block, ser_local, width = group_ref.shape
@@ -144,8 +145,8 @@
             full_ref[pl.ds(to, quarter)] = part[...]
 
     group = jnp.swapaxes(group_ref[...].astype(jnp.float32), 0, 1).reshape(ser_local * block, width)
-    own = jnp.concatenate([own_a[...], own_b[...]], axis=0).reshape(ser_local * block, half).astype(jnp.float32)
-    other = jnp.concatenate([other_a[...], other_b[...]], axis=0).reshape(ser_local * block, half).astype(jnp.float32)
+    own = own_ref[...].reshape(ser_local * block, half).astype(jnp.float32)
+    other = other_ref[...].reshape(ser_local * block, half).astype(jnp.float32)
     is_low = me == 0
     low = jnp.where(is_low, own, other)
     high = jnp.where(is_low, other, own)
@@ -224,7 +225,6 @@
     gate_a, gate_b = from_partner(w_gate)
     out_a, out_b = from_partner(w_out)
 
-    first_count = ser_local * FIRST_SERIES[0] // FIRST_SERIES[1]
     time_own, time_other = [], []
 
     def time_call(at, count, after):
@@ -253,13 +253,10 @@
         time_own.append(own)
 
     send_chunk(1, (sent[0],))
-    time_call(0, first_count, (sent[1],))
-    send_chunk(2, (time_own[0],))
-    time_call(first_count, ser_local - first_count, (sent[2], group_a, gate_a, out_a))
-
-    counts = [first_count, ser_local - first_count]
+    time_call(0, ser_local, (sent[1],))
+    counts = [ser_local]
     out = jnp.zeros((ser_local, patches, width), jnp.bfloat16)
-    last = time_own[1]
+    last = time_own[-1]
     backs = []
     for c, step in enumerate(steps):
         call = pl.pallas_call(

time: 287 us -> 234 us (0.82)
  blocking collectives: 35.6 us -> 0 us
  waiting for transfers between devices: 112 us -> 101 us
  Pallas kernels: 87.5 us -> 78.5 us
    all_to_all x1 -> x0, blocking collectives: 35.6 us -> none  [split_patches(): lax.all_to_all(group_out, 'series', split_axis=0, concat_axis=0, tiled=True)]
    ppermute x2 -> x1, waiting for transfers between devices: 33 us -> 0.01 us  [time_call(): time_other.append(lax.ppermute(give, 'mp', swap))]
    all_to_all x2, waiting for transfers between devices: 15.6 us -> 27.6 us  [split_patches(): lax.all_to_all(group_out, 'series', split_axis=0, concat_axis=0, tiled=True)]
    all_to_all x3 -> x2, waiting for transfers between devices: 21.4 us -> 31.4 us  [send_chunk(): lax.all_to_all(piece.reshape(ns, step, ser_local, depth), 'series', split...]
    all_to_all x2, starting transfers between devices: 11.1 us -> 16.5 us  [split_patches(): lax.all_to_all(group_out, 'series', split_axis=0, concat_axis=0, tiled=True)]
    pallas_call x3 -> x2, Pallas kernels: 34 us -> 30.4 us  [split_patches(): call(received[c], group_own, group_a, group_b, w_gate, gate_a, gate_b, gr...]
    ppermute x3 -> x2, waiting for transfers between devices: 21.5 us -> 24.8 us  [split_patches(): taken = lax.ppermute(give, 'mp', swap)]
    all_to_all x3 -> x2, starting transfers between devices: 20.8 us -> 18.1 us  [send_chunk(): lax.all_to_all(piece.reshape(ns, step, ser_local, depth), 'series', split...]
  transfers between devices with their start and end apart: 16 -> 13, of which waited for: 8 -> 8; matrix products, arithmetic and copies ran while one was open for 2% -> 3% of each run, Pallas kernels for 29% -> 32%
where the time goes in v4:
time: 234 us; the launch traced here: 233 us
  waiting for transfers between devices  101 us (43%)
  Pallas kernels  78.5 us (34%)
  starting transfers between devices  44.3 us (19%)
  local copies, waits for them, and re-layouts  8.7 us (4%)
    all_to_all x2, waiting for transfers between devices, send_chunk(): lax.all_to_all(piece.reshape(ns, step, ser_local, depth), 'series', split...  31.4 us
    pallas_call x2, Pallas kernels, split_patches(): call(received[c], group_own, group_a, group_b, w_gate, gate_a, gate_b, gr...  30.4 us
    all_to_all x2, waiting for transfers between devices, split_patches(): lax.all_to_all(group_out, 'series', split_axis=0, concat_axis=0, tiled=True)  27.6 us
    pallas_call x1, Pallas kernels, time_call(): own, give = call(series_in, norm_gain, turned(w_time), *after)  27.2 us
    ppermute x2, waiting for transfers between devices, split_patches(): taken = lax.ppermute(give, 'mp', swap)  24.8 us
    all_to_all x2, starting transfers between devices, send_chunk(): lax.all_to_all(piece.reshape(ns, step, ser_local, depth), 'series', split...  18.1 us
    all_to_all x2, starting transfers between devices, split_patches(): lax.all_to_all(group_out, 'series', split_axis=0, concat_axis=0, tiled=True)  16.5 us
    ppermute x3, waiting for transfers between devices, from_partner(): first = lax.ppermute(part, 'mp', swap)  15.6 us
  transfers between devices with their start and end apart: 13, of which 8 were waited for; matrix products, arithmetic and copies ran while one was open for 3% of the time, Pallas kernels for 32%

profile of v4, /device:TPU:0, one launch (start us, length us, event | category | flops | bytes accessed | tf_op | source)
XLA Modules:
  0.0 232.7 jit_solution(15973809651176182119)
XLA Ops:
  0.0 5.2 %prep_path.2.rest_0_ = bf16[80,16,768]{2,1,0:T(8,128)(2,1)} custom-call(s32[1]{0:T(128)} %bitcast._, bf16[16,256,768]{2,1,0:T(8,128)(2,1)} %x_ref.5, f32[768]{0:T(1024)} %gain_ref.5), custom_call_target="tpu_custom_call" | custom-call | tf_op jit(solution)/shard_map/prep_path/pallas_call | solution.py:193
  5.2 7.4 %all-to-all-start = ((bf16[16,5,16,768]{3,2,1,0:T(8,128)(2,1)}), bf16[16,5,16,768]{3,2,1,0:T(8,128)(2,1)S(1)}, u32[]{:S(2)}, u32[]{:S(2)}) async-start(bf16[16,5,16,768]{3,2,1,0:T(8,128)(2,1)} %bitcast.11), calls=%async_computation | async-start | bytes 3932160 | tf_op jit(solution)/shard_map/all_to_all | solution.py:214
  12.6 2.2 dynamic-slice_bitcast_fusion
  16.3 3.6 %prep_path.3.rest_0_ = bf16[48,16,768]{2,1,0:T(8,128)(2,1)} custom-call(s32[1]{0:T(128)} %bitcast._, bf16[16,256,768]{2,1,0:T(8,128)(2,1)} %x_ref.5, f32[768]{0:T(1024)} %gain_ref.5, bf16[80,16,768]{2,1,0:T(8,128)(2,1)} %prep_path.2.rest_0_), custom_call_target="tpu_custom_call" | custom-call | tf_op jit(solution)/shard_map/prep_path/pallas_call | solution.py:193
  19.9 31.4 %all-to-all-done.x_ref = bf16[16,5,16,768]{3,2,1,0:T(8,128)(2,1)S(1)} async-done(((bf16[16,5,16,768]{3,2,1,0:T(8,128)(2,1)}), bf16[16,5,16,768]{3,2,1,0:T(8,128)(2,1)S(1)}, u32[]{:S(2)}, u32[]{:S(2)}) %all-to-all-start) | async-done | bytes 1966112 | tf_op jit(solution)/shard_map/all_to_all | solution.py:214
  51.3 10.7 %all-to-all-start.2 = ((bf16[16,3,16,768]{3,2,1,0:T(8,128)(2,1)}), bf16[16,3,16,768]{3,2,1,0:T(8,128)(2,1)S(1)}, u32[]{:S(2)}, u32[]{:S(2)}) async-start(bf16[16,3,16,768]{3,2,1,0:T(8,128)(2,1)} %bitcast.13), calls=%async_computation.2 | async-start | bytes 2359296 | tf_op jit(solution)/shard_map/all_to_all | solution.py:214
  63.0 1.6 collective-permute-start.2
  64.6 7.8 %collective-permute-done.2.ga_ref = bf16[384,384]{1,0:T(8,128)(2,1)S(1)} collective-permute-done((bf16[384,384]{1,0:T(8,128)(2,1)S(1)}, bf16[384,384]{1,0:T(8,128)(2,1)S(1)}, u32[]{:S(2)}, u32[]{:S(2)}) %collective-permute-start.2) | collective-permute-done | bytes 294944 | tf_op jit(solution)/shard_map/ppermute | solution.py:182
  72.9 27.2 %time_path.1 = (bf16[16,128,384]{2,1,0:T(8,128)(2,1)}, bf16[16,128,384]{2,1,0:T(8,128)(2,1)}) custom-call(bf16[16,256,768]{2,1,0:T(8,128)(2,1)} %x_ref.5, f32[768]{0:T(1024)} %gain_ref.5, bf16[6,192,768]{2,1,0:T(8,128)(2,1)} %bitcast.19, bf16[48,16,768]{2,1,0:T(8,128)(2,1)} %prep_path.3.rest_0_), custom_call_target="tpu_custom_call" | custom-call | flops 10468982784 | bytes 9437184 | tf_op jit(solution)/shard_map/time_path/pallas_call | solution.py:251
  100.9 18.1 %group_path.2._ = bf16[16,5,16,768]{3,2,1,0:T(8,128)(2,1)} custom-call(bf16[16,5,16,768]{3,2,1,0:T(8,128)(2,1)} %copy-done.3, bf16[6,192,768]{2,1,0:T(8,128)(2,1)} %bitcast.14, bf16[3,192,768]{2,1,0:T(8,128)(2,1)} %collective-permute-done.wa_ref, bf16[3,192,768]{2,1,0:T(8,128)(2,1)} %collective-permute-done.1.wb_ref, bf16[768,384]{1,0:T(8,128)(2,1)} %g_ref.3, ...), custom_call_target="tpu_custom_call" | custom-call | flops 8053063680 | bytes 3932160 | tf_op jit(solution)/shard_map/group_path/pallas_call | solution.py:291
  119.1 5.8 %all-to-all-start.1 = ((bf16[16,5,16,768]{3,2,1,0:T(8,128)(2,1)}), bf16[16,5,16,768]{3,2,1,0:T(8,128)(2,1)S(1)}, u32[]{:S(2)}, u32[]{:S(2)}) async-start(bf16[16,5,16,768]{3,2,1,0:T(8,128)(2,1)} %group_path.2._), calls=%async_computation.1 | async-start | bytes 3932160 | tf_op jit(solution)/shard_map/all_to_all | solution.py:296
  124.9 1.6 collective-permute-start.4
  126.4 12.3 %group_path.3 = bf16[16,3,16,768]{3,2,1,0:T(8,128)(2,1)} custom-call(bf16[16,3,16,768]{3,2,1,0:T(8,128)(2,1)} %copy-done.4, bf16[6,192,768]{2,1,0:T(8,128)(2,1)} %bitcast.15, bf16[3,192,768]{2,1,0:T(8,128)(2,1)} %collective-permute-done.wa_ref, bf16[3,192,768]{2,1,0:T(8,128)(2,1)} %collective-permute-done.1.wb_ref, bf16[768,384]{1,0:T(8,128)(2,1)} %g_ref.3, ...), custom_call_target="tpu_custom_call" | custom-call | flops 4831838208 | bytes 2359296 | tf_op jit(solution)/shard_map/group_path/pallas_call | solution.py:291
  138.7 24.9 %all-to-all-done.1 = bf16[16,5,16,768]{3,2,1,0:T(8,128)(2,1)S(1)} async-done(((bf16[16,5,16,768]{3,2,1,0:T(8,128)(2,1)}), bf16[16,5,16,768]{3,2,1,0:T(8,128)(2,1)S(1)}, u32[]{:S(2)}, u32[]{:S(2)}) %all-to-all-start.1) | async-done | bytes 1966112 | tf_op jit(solution)/shard_map/all_to_all | solution.py:296
  163.5 10.7 %all-to-all-start.3 = ((bf16[16,3,16,768]{3,2,1,0:T(8,128)(2,1)}), bf16[16,3,16,768]{3,2,1,0:T(8,128)(2,1)}, u32[]{:S(2)}, u32[]{:S(2)}) async-start(bf16[16,3,16,768]{3,2,1,0:T(8,128)(2,1)} %group_path.3), calls=%async_computation.3 | async-start | bytes 2359296 | tf_op jit(solution)/shard_map/all_to_all | solution.py:296
  175.3 1.6 collective-permute-start.5
  176.9 7.8 %collective-permute-done.5.wa_ref = bf16[192,768]{1,0:T(8,128)(2,1)S(1)} collective-permute-done((bf16[192,768]{1,0:T(8,128)(2,1)S(1)}, bf16[192,768]{1,0:T(8,128)(2,1)S(1)}, u32[]{:S(2)}, u32[]{:S(2)}) %collective-permute-start.5) | collective-permute-done | bytes 294944 | tf_op jit(solution)/shard_map/ppermute | solution.py:182
  184.6 1.6 collective-permute-done.6.wb_ref
  188.1 7.0 %join_path.2 = (bf16[16,80,384]{2,1,0:T(8,128)(2,1)}, bf16[16,80,384]{2,1,0:T(8,128)(2,1)}) custom-call(bf16[80,16,768]{2,1,0:T(8,128)(2,1)} %bitcast.12, bf16[16,128,384]{2,1,0:T(8,128)(2,1)} %get-tuple-element.11._.own_ref, bf16[16,128,384]{2,1,0:T(8,128)(2,1)} %copy-done.1, bf16[384,768]{1,0:T(8,128)(2,1)} %w_ref.3, bf16[192,768]{1,0:T(8,128)(2,1)} %copy-done.5, ...), custom_call_target="tpu_custom_call" | custom-call | flops 1509949440 | bytes 7864320 | tf_op jit(solution)/shard_map/join_path/pallas_call | solution.py:323
  195.2 1.5 collective-permute-start.7
  196.7 2.7 %all-to-all-done.3 = bf16[16,3,16,768]{3,2,1,0:T(8,128)(2,1)} async-done(((bf16[16,3,16,768]{3,2,1,0:T(8,128)(2,1)}), bf16[16,3,16,768]{3,2,1,0:T(8,128)(2,1)}, u32[]{:S(2)}, u32[]{:S(2)}) %all-to-all-start.3) | async-done | bytes 1179680 | tf_op jit(solution)/shard_map/all_to_all | solution.py:296
  199.4 5.1 %join_path.3 = (bf16[16,48,384]{2,1,0:T(8,128)(2,1)}, bf16[16,48,384]{2,1,0:T(8,128)(2,1)}) custom-call(bf16[48,16,768]{2,1,0:T(8,128)(2,1)} %bitcast.9.group_ref, bf16[16,128,384]{2,1,0:T(8,128)(2,1)} %get-tuple-element.11._.own_ref, bf16[16,128,384]{2,1,0:T(8,128)(2,1)} %copy-done.1, bf16[384,768]{1,0:T(8,128)(2,1)} %w_ref.3, bf16[192,768]{1,0:T(8,128)(2,1)} %copy-done.5, ...), custom_call_target="tpu_custom_call" | custom-call | flops 905969664 | bytes 4718592 | tf_op jit(solution)/shard_map/join_path/pallas_call | solution.py:323
  206.6 13.4 %collective-permute-done.7 = bf16[16,80,384]{2,1,0:T(8,128)(2,1)S(1)} collective-permute-done((bf16[16,80,384]{2,1,0:T(8,128)(2,1)}, bf16[16,80,384]{2,1,0:T(8,128)(2,1)S(1)}, u32[]{:S(2)}, u32[]{:S(2)}) %collective-permute-start.7) | collective-permute-done | bytes 983072 | tf_op jit(solution)/shard_map/ppermute | solution.py:324
  220.3 11.5 %collective-permute-done.8 = bf16[16,48,384]{2,1,0:T(8,128)(2,1)S(1)} collective-permute-done((bf16[16,48,384]{2,1,0:T(8,128)(2,1)}, bf16[16,48,384]{2,1,0:T(8,128)(2,1)S(1)}, u32[]{:S(2)}, u32[]{:S(2)}) %collective-permute-start.8) | collective-permute-done | bytes 589856 | tf_op jit(solution)/shard_map/ppermute | solution.py:324
  (40 shorter events, 10.0 us)
Async XLA Ops:
  5.2 46.1 %all-to-all-start = ((bf16[16,5,16,768]{3,2,1,0:T(8,128)(2,1)}), bf16[16,5,16,768]{3,2,1,0:T(8,128)(2,1)S(1)}, u32[]{:S(2)}, u32[]{:S(2)}) async-start(bf16[16,5,16,768]{3,2,1,0:T(8,128)(2,1)} %bitcast.11), calls=%async_computation | async-start | bytes 3932160 | tf_op jit(solution)/shard_map/all_to_all | solution.py:214
  14.8 57.6 %collective-permute-start = (bf16[3,192,768]{2,1,0:T(8,128)(2,1)}, bf16[3,192,768]{2,1,0:T(8,128)(2,1)}, u32[]{:S(2)}, u32[]{:S(2)}) collective-permute-start(bf16[3,192,768]{2,1,0:T(8,128)(2,1)} %dynamic-slice_bitcast_fusion), channel_id=1, source_target_pairs={{0,1},{1,0},{2,3},{3,2},{4,5},{5,4},{6,7},{7,6},{8,9},{9,8},{10,11... | collective-permute-start | bytes 2654216 | tf_op jit(solution)/shard_map/ppermute | solution.py:182
  51.3 48.8 %copy-start.3 = (bf16[16,5,16,768]{3,2,1,0:T(8,128)(2,1)}, bf16[16,5,16,768]{3,2,1,0:T(8,128)(2,1)S(1)}, u32[]{:S(2)}) copy-start(bf16[16,5,16,768]{3,2,1,0:T(8,128)(2,1)S(1)} %all-to-all-done.x_ref) | copy-start | bytes 5898244
  51.3 67.8 %all-to-all-start.2 = ((bf16[16,3,16,768]{3,2,1,0:T(8,128)(2,1)}), bf16[16,3,16,768]{3,2,1,0:T(8,128)(2,1)S(1)}, u32[]{:S(2)}, u32[]{:S(2)}) async-start(bf16[16,3,16,768]{3,2,1,0:T(8,128)(2,1)} %bitcast.13), calls=%async_computation.2 | async-start | bytes 2359296 | tf_op jit(solution)/shard_map/all_to_all | solution.py:214
  63.0 9.4 %collective-permute-start.2 = (bf16[384,384]{1,0:T(8,128)(2,1)S(1)}, bf16[384,384]{1,0:T(8,128)(2,1)S(1)}, u32[]{:S(2)}, u32[]{:S(2)}) collective-permute-start(bf16[384,384]{1,0:T(8,128)(2,1)S(1)} %constant_dynamic-slice_fusion.1), channel_id=1, source_target_pairs={{0,1},{1,0},{2,3},{3,2},{4,5},{5,4},{6,7},{7,6},{8,9},{9,8},{10,11... | collective-permute-start | bytes 884744 | tf_op jit(solution)/shard_map/ppermute | solution.py:182
  72.4 27.7 %copy-start.10 = (bf16[384,384]{1,0:T(8,128)(2,1)}, bf16[384,384]{1,0:T(8,128)(2,1)S(1)}, u32[]{:S(2)}) copy-start(bf16[384,384]{1,0:T(8,128)(2,1)S(1)} %collective-permute-done.2.ga_ref) | copy-start | bytes 884740
  72.4 28.6 %collective-permute-start.3 = (bf16[384,384]{1,0:T(8,128)(2,1)S(1)}, bf16[384,384]{1,0:T(8,128)(2,1)}, u32[]{:S(2)}, u32[]{:S(2)}) collective-permute-start(bf16[384,384]{1,0:T(8,128)(2,1)S(1)} %collective-permute-done.2.ga_ref), channel_id=1, source_target_pairs={{0,2},{2,0},{4,6},{6,4},{8,10},{10,8},{12,14},{14,12},{16,18},{18,... | collective-permute-start | bytes 884744 | tf_op jit(solution)/shard_map/ppermute | solution.py:183
  72.4 28.6 %collective-permute-start.1 = (bf16[3,192,768]{2,1,0:T(8,128)(2,1)}, bf16[3,192,768]{2,1,0:T(8,128)(2,1)}, u32[]{:S(2)}, u32[]{:S(2)}) collective-permute-start(bf16[3,192,768]{2,1,0:T(8,128)(2,1)} %collective-permute-done.wa_ref), channel_id=1, source_target_pairs={{0,2},{2,0},{4,6},{6,4},{8,10},{10,8},{12,14},{14,12},{16,18},{18,... | collective-permute-start | bytes 2654216 | tf_op jit(solution)/shard_map/ppermute | solution.py:183
  72.9 27.2 %copy-start.9 = (s32[256]{0:T(256)S(1)}, s32[256]{0:T(256)}, u32[]{:S(2)}) copy-start(s32[256]{0:T(256)} %param.13) | copy-start | bytes 3076
  119.1 5.8 %copy-start.4 = (bf16[16,3,16,768]{3,2,1,0:T(8,128)(2,1)}, bf16[16,3,16,768]{3,2,1,0:T(8,128)(2,1)S(1)}, u32[]{:S(2)}) copy-start(bf16[16,3,16,768]{3,2,1,0:T(8,128)(2,1)S(1)} %all-to-all-done.2.x_ref) | copy-start | bytes 3538948
  119.1 44.5 %all-to-all-start.1 = ((bf16[16,5,16,768]{3,2,1,0:T(8,128)(2,1)}), bf16[16,5,16,768]{3,2,1,0:T(8,128)(2,1)S(1)}, u32[]{:S(2)}, u32[]{:S(2)}) async-start(bf16[16,5,16,768]{3,2,1,0:T(8,128)(2,1)} %group_path.2._), calls=%async_computation.1 | async-start | bytes 3932160 | tf_op jit(solution)/shard_map/all_to_all | solution.py:296
  124.9 61.3 %collective-permute-start.4 = (bf16[16,128,384]{2,1,0:T(8,128)(2,1)}, bf16[16,128,384]{2,1,0:T(8,128)(2,1)S(1)}, u32[]{:S(2)}, u32[]{:S(2)}) collective-permute-start(bf16[16,128,384]{2,1,0:T(8,128)(2,1)} %get-tuple-element.12), channel_id=1, source_target_pairs={{0,1},{1,0},{2,3},{3,2},{4,5},{5,4},{6,7},{7,6},{8,9},{9,8},{10,11... | collective-permute-start | bytes 4718600 | tf_op jit(solution)/shard_map/ppermute | solution.py:252
  163.5 23.4 %copy-start = (bf16[16,5,16,768]{3,2,1,0:T(8,128)(2,1)}, bf16[16,5,16,768]{3,2,1,0:T(8,128)(2,1)S(1)}, u32[]{:S(2)}) copy-start(bf16[16,5,16,768]{3,2,1,0:T(8,128)(2,1)S(1)} %all-to-all-done.1) | copy-start | bytes 5898244
  163.5 35.8 %all-to-all-start.3 = ((bf16[16,3,16,768]{3,2,1,0:T(8,128)(2,1)}), bf16[16,3,16,768]{3,2,1,0:T(8,128)(2,1)}, u32[]{:S(2)}, u32[]{:S(2)}) async-start(bf16[16,3,16,768]{3,2,1,0:T(8,128)(2,1)} %group_path.3), calls=%async_computation.3 | async-start | bytes 2359296 | tf_op jit(solution)/shard_map/all_to_all | solution.py:296
  175.3 9.3 %collective-permute-start.5 = (bf16[192,768]{1,0:T(8,128)(2,1)S(1)}, bf16[192,768]{1,0:T(8,128)(2,1)S(1)}, u32[]{:S(2)}, u32[]{:S(2)}) collective-permute-start(bf16[192,768]{1,0:T(8,128)(2,1)S(1)} %constant_dynamic-slice_fusion), channel_id=1, source_target_pairs={{0,1},{1,0},{2,3},{3,2},{4,5},{5,4},{6,7},{7,6},{8,9},{9,8},{10,11... | collective-permute-start | bytes 884744 | tf_op jit(solution)/shard_map/ppermute | solution.py:182
  184.6 2.3 %copy-start.5 = (bf16[192,768]{1,0:T(8,128)(2,1)}, bf16[192,768]{1,0:T(8,128)(2,1)S(1)}, u32[]{:S(2)}) copy-start(bf16[192,768]{1,0:T(8,128)(2,1)S(1)} %collective-permute-done.5.wa_ref) | copy-start | bytes 884740
  184.6 1.6 collective-permute-start.6
  186.2 0.7 copy-start.6
  186.9 1.2 copy-start.1
  195.2 24.8 %collective-permute-start.7 = (bf16[16,80,384]{2,1,0:T(8,128)(2,1)}, bf16[16,80,384]{2,1,0:T(8,128)(2,1)S(1)}, u32[]{:S(2)}, u32[]{:S(2)}) collective-permute-start(bf16[16,80,384]{2,1,0:T(8,128)(2,1)} %get-tuple-element.14), channel_id=1, source_target_pairs={{0,1},{1,0},{2,3},{3,2},{4,5},{5,4},{6,7},{7,6},{8,9},{9,8},{10,11... | collective-permute-start | bytes 2949128 | tf_op jit(solution)/shard_map/ppermute | solution.py:324
  199.4 7.0 %copy-start.7 = (bf16[16,80,384]{2,1,0:T(8,128)(2,1)S(1)}, bf16[16,80,384]{2,1,0:T(8,128)(2,1)}, u32[]{:S(2)}) copy-start(bf16[16,80,384]{2,1,0:T(8,128)(2,1)} %get-tuple-element.13) | copy-start | bytes 2949124
  204.5 27.3 %collective-permute-start.8 = (bf16[16,48,384]{2,1,0:T(8,128)(2,1)}, bf16[16,48,384]{2,1,0:T(8,128)(2,1)S(1)}, u32[]{:S(2)}, u32[]{:S(2)}) collective-permute-start(bf16[16,48,384]{2,1,0:T(8,128)(2,1)} %get-tuple-element.16), channel_id=1, source_target_pairs={{0,1},{1,0},{2,3},{3,2},{4,5},{5,4},{6,7},{7,6},{8,9},{9,8},{10,11... | collective-permute-start | bytes 1769480 | tf_op jit(solution)/shard_map/ppermute | solution.py:324
  206.0 14.2 %copy-start.8 = (bf16[16,48,384]{2,1,0:T(8,128)(2,1)S(1)}, bf16[16,48,384]{2,1,0:T(8,128)(2,1)}, u32[]{:S(2)}) copy-start(bf16[16,48,384]{2,1,0:T(8,128)(2,1)} %get-tuple-element.15) | copy-start | bytes 1769476
  220.3 11.5 %copy-start.2 = (bf16[16,256,384]{2,1,0:T(8,128)(2,1)}, bf16[16,256,384]{2,1,0:T(8,128)(2,1)S(1)}, u32[]{:S(2)}) copy-start(bf16[16,256,384]{2,1,0:T(8,128)(2,1)S(1)} %constant_dynamic-update-slice_fusion.1) | copy-start | bytes 9437188
